TPU v7x, 768 devices: a whole 4x8x12 slice. The times are simulated.
768 devices in a mesh: dp: 48 (over z, x_lo, core), pipe: 16 (over x_hi, y).
Axes of the slice: x: 4 (x_hi: 2, x_lo: 2; x = x_hi * 2 + x_lo), y: 8, z: 12, core: 2. Of those that a mesh axis runs over, the one named last changes fastest.
Arguments:
- acts_fwd: bfloat16 [16, 6144, 768], P('pipe', 'dp'), may hold values from -6 to 6
- acts_bwd: bfloat16 [16, 6144, 768], P('pipe', 'dp'), may hold values from -6 to 6
- cotangent: bfloat16 [16, 6144, 768], P('pipe', 'dp'), may hold values from -6 to 6
- lens_fwd: int32 [16, 48, 4], P('pipe', 'dp'), may hold values from 1 to 64, 128 in all within a row
- lens_bwd: int32 [16, 48, 4], P('pipe', 'dp'), may hold values from 1 to 64, 128 in all within a row
- w_proj: float32 [16, 768, 2048], P('pipe', 'dp'), may hold values from -0.21875 to 0.21875
- w_out: float32 [16, 512, 768], P('pipe', None, 'dp'), may hold values from -0.25 to 0.25
Outputs:
- next_acts: bfloat16 [16, 6144, 768], P('pipe', 'dp')
- prev_grads: bfloat16 [16, 6144, 768], P('pipe', 'dp')
- grad_proj: float32 [16, 768, 2048], P('pipe', 'dp')
- grad_out: float32 [16, 512, 768], P('pipe', None, 'dp')
Inputs may be any that keep to these rules, and one draw needn't show every extreme that they name: `lens_fwd`: each row of 4 lengths sums to 128; its largest is exactly 64. `lens_bwd`: each row of 4 lengths sums to 128; its largest is exactly 64.
All inputs are finite; a program needn't handle non-finite values.
Results may differ from a plain program's by a relative error of at most 0.011.
Values may be sent and summed in bfloat16 or wider, within the bound.
No kernel may reach another device: no remote copies, remote signals or barrier semaphores. Data moves between devices by JAX's collectives and lax.ppermute only.
A program may use at most 32 MiB of HBM per device.

v0:
```python
import math

import jax
import jax.numpy as jnp
from jax import lax
from jax.sharding import PartitionSpec as P

HEADS = 4
HEAD_DIM = 128
HID = 512
LMAX = 64


EPS = 1e-05


def passed_along(array, axis, by):
    count = lax.axis_size(axis)
    return lax.ppermute(array, axis, [(i, (i + by) % count) for i in range(count)])


def jagged_mask(lengths, count):
    ends = jnp.cumsum(lengths)
    positions = jnp.arange(count, dtype=jnp.int32)
    segment = jnp.sum((positions[:, None] >= ends[None, :]).astype(jnp.int32), axis=1)
    keep = (segment[:, None] == segment[None, :]) & (positions[:, None] >= positions[None, :])
    return keep.astype(jnp.float32)


def layer_norm(values):
    center = values - jnp.mean(values, axis=-1, keepdims=True)
    inverse = lax.rsqrt(jnp.mean(center * center, axis=-1, keepdims=True) + EPS)
    return (center * inverse, inverse)


def norm_back(grad_normed, normed, inverse):
    return inverse * (
        grad_normed
        - jnp.mean(grad_normed, axis=-1, keepdims=True)
        - normed * jnp.mean(grad_normed * normed, axis=-1, keepdims=True)
    )


def silu_slope(values):
    sigma = jax.nn.sigmoid(values)
    return sigma * (1.0 + values * (1.0 - sigma))


def forward_parts(tokens, w_first, keep):
    count = tokens.shape[0]
    tok_float = tokens.astype(jnp.float32)
    normed, inverse = layer_norm(tok_float)
    normed_bf = normed.astype(jnp.bfloat16)
    preact = jnp.dot(normed_bf, w_first, preferred_element_type=jnp.float32)
    hidden = jax.nn.silu(preact).astype(jnp.bfloat16)
    gate_u = hidden[:, :HID]
    values_h = hidden[:, HID : 2 * HID].reshape(count, HEADS, HEAD_DIM)
    queries = hidden[:, 2 * HID : 3 * HID].reshape(count, HEADS, HEAD_DIM)
    keys_h = hidden[:, 3 * HID :].reshape(count, HEADS, HEAD_DIM)
    scores = jnp.einsum(
        "ihd,jhd->hij", queries, keys_h, preferred_element_type=jnp.float32
    ) * HEAD_DIM ** (-0.5)
    attn = (jax.nn.silu(scores) * keep[None] * (1.0 / LMAX)).astype(jnp.bfloat16)
    mixed = jnp.einsum("hij,jhd->ihd", attn, values_h, preferred_element_type=jnp.float32).reshape(
        count, HID
    )
    mixed_n, inverse_o = layer_norm(mixed)
    gated = (mixed_n * gate_u.astype(jnp.float32)).astype(jnp.bfloat16)
    return (
        tok_float,
        normed,
        inverse,
        normed_bf,
        preact,
        gate_u,
        values_h,
        queries,
        keys_h,
        scores,
        attn,
        mixed_n,
        inverse_o,
        gated,
    )


def forward(tokens, w_first, w_second, keep):
    parts = forward_parts(tokens, w_first, keep)
    return (parts[0] + jnp.dot(parts[13], w_second, preferred_element_type=jnp.float32)).astype(
        jnp.bfloat16
    )


def backward(tokens, cotan, w_first, w_second, keep):
    count = tokens.shape[0]
    (
        tok_float,
        normed,
        inverse,
        normed_bf,
        preact,
        gate_u,
        values_h,
        queries,
        keys_h,
        scores,
        attn,
        mixed_n,
        inverse_o,
        gated,
    ) = forward_parts(tokens, w_first, keep)
    grad_y = jnp.dot(cotan, w_second.T, preferred_element_type=jnp.float32)
    grad_u = grad_y * mixed_n
    grad_mn = grad_y * gate_u.astype(jnp.float32)
    grad_mixed = (
        norm_back(grad_mn, mixed_n, inverse_o).astype(jnp.bfloat16).reshape(count, HEADS, HEAD_DIM)
    )
    grad_attn = jnp.einsum("ihd,jhd->hij", grad_mixed, values_h, preferred_element_type=jnp.float32)
    grad_vals = jnp.einsum("hij,ihd->jhd", attn, grad_mixed, preferred_element_type=jnp.float32)
    grad_scores = (
        grad_attn * keep[None] * (1.0 / LMAX) * silu_slope(scores) * HEAD_DIM ** (-0.5)
    ).astype(jnp.bfloat16)
    grad_q = jnp.einsum("hij,jhd->ihd", grad_scores, keys_h, preferred_element_type=jnp.float32)
    grad_k = jnp.einsum("hij,ihd->jhd", grad_scores, queries, preferred_element_type=jnp.float32)
    grad_hidden = jnp.concatenate(
        [
            grad_u,
            grad_vals.reshape(count, HID),
            grad_q.reshape(count, HID),
            grad_k.reshape(count, HID),
        ],
        axis=1,
    )
    grad_pre = (grad_hidden * silu_slope(preact)).astype(jnp.bfloat16)
    grad_norm = jnp.dot(grad_pre, w_first.T, preferred_element_type=jnp.float32)
    grad_in = (cotan.astype(jnp.float32) + norm_back(grad_norm, normed, inverse)).astype(
        jnp.bfloat16
    )
    return (grad_in, normed_bf, grad_pre, gated)


def per_device(acts_fwd, acts_bwd, cotangent, lens_fwd, lens_bwd, w_proj, w_out):
    w_first, w_second = (
        lax.all_gather(w_proj[0].astype(jnp.bfloat16), "dp", axis=0, tiled=True),
        lax.all_gather(w_out[0].astype(jnp.bfloat16), "dp", axis=1, tiled=True),
    )
    block_rows = acts_fwd.shape[1]
    loss_scale = 1.0 / math.sqrt(lax.axis_size("dp") * block_rows)
    result = forward(acts_fwd[0], w_first, w_second, jagged_mask(lens_fwd[0, 0], block_rows))
    forward_out = passed_along(result, "pipe", 1)[None]
    cotan = cotangent[0]
    grad_in, normed_bf, grad_pre, gated = backward(
        acts_bwd[0], cotan, w_first, w_second, jagged_mask(lens_bwd[0, 0], block_rows)
    )
    term_proj = jnp.dot(normed_bf.T, grad_pre, preferred_element_type=jnp.float32) * loss_scale
    term_out = jnp.dot(gated.T, cotan, preferred_element_type=jnp.float32) * loss_scale
    summed_proj = lax.psum_scatter(term_proj, "dp", scatter_dimension=0, tiled=True)
    summed_out = lax.psum_scatter(term_out, "dp", scatter_dimension=1, tiled=True)
    arrived = passed_along(grad_in, "pipe", -1)
    return (forward_out, arrived[None], summed_proj[None], summed_out[None])


def solution(mesh):
    return jax.shard_map(
        per_device,
        mesh=mesh,
        in_specs=(
            P("pipe", "dp", None),
            P("pipe", "dp", None),
            P("pipe", "dp", None),
            P("pipe", "dp", None),
            P("pipe", "dp", None),
            P("pipe", "dp", None),
            P("pipe", None, "dp"),
        ),
        out_specs=(
            P("pipe", "dp", None),
            P("pipe", "dp", None),
            P("pipe", "dp", None),
            P("pipe", None, "dp"),
        ),
        check_vma=False,
    )
```

profile of v0, /device:TPU:24, one launch (start us, length us, event | category | flops | bytes accessed | tf_op | source)
XLA Modules:
  0.0 495.3 jit_solution(17792102517671786012)
XLA Ops:
  7.2 1.5 convert_element_type.96
  8.8 0.8 reduce-window.17
  9.7 1.0 convert_reduce_fusion
  10.8 1.1 fusion.33
  12.0 103.7 %all-gather.4.cloned.1.call-done = bf16[1,768,2048]{2,1,0:T(8,128)(2,1)} async-done(((bf16[1,16,2048]{2,1,0:T(8,128)(2,1)}), bf16[1,768,2048]{2,1,0:T(8,128)(2,1)}) %all-gather.4.cloned.1.call-update) | async-done | bytes 3145744 | tf_op jit(solution)/shard_map/all_gather | solution.py:144
  115.7 2.7 multiply_convert_fusion
  119.5 1.6 convolution_multiply_fusion.1
  121.3 49.1 %all-gather.1 = bf16[1,512,768]{1,2,0:T(8,128)(2,1)S(1)} all-gather(bf16[1,512,16]{1,2,0:T(8,128)(2,1)S(1)} %convert_element_type.104), channel_id=3, replica_groups=mesh['dp'=48,'pipe'=16] {'dp'}, dimensions={2}, use_global_device_ids=true | all-gather | bytes 802816 | tf_op jit(solution)/shard_map/all_gather | solution.py:145
  170.7 0.8 fusion.45
  172.4 1.3 fusion.10
  174.4 1.3 fusion.11
  175.7 3.7 convolution_multiply_fusion
  179.5 0.6 copy-done.9
  180.8 2.6 multiply_convert_fusion.1
  183.6 0.4 fusion.87
  184.3 0.4 fusion.6
  184.7 4.6 collective-permute-start
  189.3 3.2 fusion.86
  192.7 1.9 collective-permute-start.1
  194.6 8.0 %collective-permute-done.1 = bf16[128,768]{1,0:T(8,128)(2,1)S(1)} collective-permute-done((bf16[128,768]{1,0:T(8,128)(2,1)S(1)}, bf16[128,768]{1,0:T(8,128)(2,1)S(1)}, u32[]{:S(2)}, u32[]{:S(2)}) %collective-permute-start.1) | collective-permute-done | bytes 196640 | tf_op jit(solution)/shard_map/ppermute | solution.py:19
  202.7 95.1 %reduce-scatter.5.cloned.1.call-done = f32[512,16]{0,1:T(8,128)} async-done(((f32[512,768]{0,1:T(8,128)}), f32[512,16]{0,1:T(8,128)}) %reduce-scatter.5.cloned.1.call-update) | async-done | bytes 32784 | tf_op jit(solution)/shard_map/reduce_scatter | solution.py:158
  297.8 189.6 %reduce-scatter.3.cloned.1.call-done = f32[16,2048]{1,0:T(8,128)} async-done(((f32[768,2048]{1,0:T(8,128)}), f32[16,2048]{1,0:T(8,128)}) %reduce-scatter.3.cloned.1.call-update) | async-done | bytes 131088 | tf_op jit(solution)/shard_map/reduce_scatter | solution.py:157
  487.4 0.7 copy.89
  488.1 0.7 copy.90
  (64 shorter events, 4.5 us)
Async XLA Ops:
  7.2 108.5 %all-gather.4.cloned.1.call-start = ((), (), s32[]{:S(2)}) async-start(), calls=%async_computation.4 | async-start | bytes 3211264 | tf_op jit(solution)/shard_map/all_gather | solution.py:144
  8.8 289.0 %reduce-scatter.5.cloned.1.call-start = ((), (), s32[]{:S(2)}) async-start(), calls=%async_computation.3 | async-start | bytes 1605632 | tf_op jit(solution)/shard_map/reduce_scatter | solution.py:158
  12.0 106.9 %copy-start.6 = (f32[128,128]{1,0:T(8,128)}, f32[128,128]{1,0:T(8,128)S(1)}, u32[]{:S(2)}) copy-start(f32[128,128]{1,0:T(8,128)S(1)} %fusion.80) | copy-start | bytes 196612
  118.4 1.1 copy-start.2
  118.4 0.9 copy-start.4
  118.7 2.5 copy-start.8
  119.0 52.9 %copy-start.3 = (f32[4,128,128]{2,1,0:T(8,128)}, f32[4,128,128]{2,1,0:T(8,128)S(1)}, u32[]{:S(2)}) copy-start(f32[4,128,128]{2,1,0:T(8,128)S(1)} %convolution_multiply_fusion.3) | copy-start | bytes 786436
  119.5 52.0 %copy-start.7 = (f32[128,128]{1,0:T(8,128)S(1)}, f32[128,128]{1,0:T(8,128)}, u32[]{:S(2)}) copy-start(f32[128,128]{1,0:T(8,128)} %copy-done.6) | copy-start | bytes 196612
  121.2 366.2 %reduce-scatter.3.cloned.1.call-start = ((), (), s32[]{:S(2)}) async-start(), calls=%async_computation.2 | async-start | bytes 6422528 | tf_op jit(solution)/shard_map/reduce_scatter | solution.py:157
  171.6 0.7 copy-start.5
  172.4 3.3 copy-start
  179.4 0.7 copy-start.9
  179.5 0.9 copy-start.1
  184.7 10.0 %collective-permute-start = (bf16[128,768]{1,0:T(8,128)(2,1)S(1)}, bf16[128,768]{1,0:T(8,128)(2,1)S(1)}, u32[]{:S(2)}, u32[]{:S(2)}) collective-permute-start(bf16[128,768]{1,0:T(8,128)(2,1)S(1)} %fusion.6), channel_id=1, source_target_pairs={{0,1},{1,2},{2,3},{3,4},{4,5},{5,6},{6,7},{7,8},{8,9},{9,10},{10,1... | collective-permute-start | bytes 589832 | tf_op jit(solution)/shard_map/ppermute | solution.py:19
  192.7 10.0 %collective-permute-start.1 = (bf16[128,768]{1,0:T(8,128)(2,1)S(1)}, bf16[128,768]{1,0:T(8,128)(2,1)S(1)}, u32[]{:S(2)}, u32[]{:S(2)}) collective-permute-start(bf16[128,768]{1,0:T(8,128)(2,1)S(1)} %fusion.32), channel_id=1, source_target_pairs={{0,15},{1,0},{2,1},{3,2},{4,3},{5,4},{6,5},{7,6},{8,7},{9,8},{10,9... | collective-permute-start | bytes 589832 | tf_op jit(solution)/shard_map/ppermute | solution.py:19
Sparse Core Ops, SparseCore 0:
  11.0 104.6 all-gather.3
  121.3 176.4 reduce-scatter.4
  301.5 185.8 reduce-scatter.2
where the time goes:
time: 496 us; the launch traced here: 495 us
  waiting for transfers between devices  396 us (80%)
  blocking collectives  49.1 us (10%)
  matrix products  17.5 us (4%)
  between operations  14.1 us (3%)
  other arithmetic  7.96 us (2%)
  starting transfers between devices  6.66 us (1%)
    reduce_scatter x1, waiting for transfers between devices, per_device(): lax.psum_scatter(term_proj, 'dp', scatter_dimension=0, tiled=True)  190 us
    all_gather x1, waiting for transfers between devices, per_device(): lax.all_gather(w_proj[0].astype(jnp.bfloat16), 'dp', axis=0, tiled=True)  104 us
    reduce_scatter x1, waiting for transfers between devices, per_device(): lax.psum_scatter(term_out, 'dp', scatter_dimension=1, tiled=True)  95.1 us
    all_gather x1, blocking collectives, per_device(): lax.all_gather(w_out[0].astype(jnp.bfloat16), 'dp', axis=1, tiled=True)  49.1 us
  transfers between devices with their start and end apart: 5, of which 4 were waited for; matrix products, arithmetic and copies ran while one was open for 4% of the time, Pallas kernels for 0%

commit v1 on v0

v1 whole, which is shorter than its diff:
```python
import math

import jax
import jax.numpy as jnp
from jax import lax
from jax.sharding import Mesh
from jax.sharding import PartitionSpec as P

HEADS = 4
HEAD_DIM = 128
HID = 512
LMAX = 64
EPS = 1e-05
Z_HIGH, Z_LOW = 4, 3
QUAD = ("x", "c")
ALONG_Z = ("zh", "zl")
ROWS = 128
BF = jnp.bfloat16
F32 = jnp.float32


def shifted(array, axis, by):
    count = lax.axis_size(axis)
    return lax.ppermute(array, axis, [(i, (i + by) % count) for i in range(count)])


def exchanged(array, axis=QUAD):
    return lax.all_to_all(array, axis, split_axis=0, concat_axis=0, tiled=True)


def after(array, *others):
    return lax.optimization_barrier((array, *others))[0]


def quad_summed(parts):
    xi, ci = lax.axis_index("x"), lax.axis_index("c")
    parts = parts.reshape(2, 2, ROWS, -1)
    arrived = shifted(lax.dynamic_index_in_dim(parts, 1 - xi, 0, False), "x", 1)
    pair = lax.dynamic_index_in_dim(parts, xi, 0, False).astype(F32) + arrived.astype(F32)
    arrived = shifted(lax.dynamic_index_in_dim(pair, 1 - ci, 0, False).astype(BF), "c", 1)
    return lax.dynamic_index_in_dim(pair, ci, 0, False) + arrived.astype(F32)


def jagged_mask(lengths):
    ends = jnp.cumsum(lengths, axis=-1)
    positions = jnp.arange(ROWS, dtype=jnp.int32)
    segment = jnp.sum(
        (positions[None, :, None] >= ends[:, None, :]).astype(jnp.int32), axis=-1
    )
    return (segment[:, :, None] == segment[:, None, :]) & (
        positions[None, :, None] >= positions[None, None, :]
    )


def layer_norm(values):
    center = values - jnp.mean(values, axis=-1, keepdims=True)
    inverse = lax.rsqrt(jnp.mean(center * center, axis=-1, keepdims=True) + EPS)
    return (center * inverse, inverse)


def silu_slope(values):
    sigma = jax.nn.sigmoid(values)
    return sigma * (1.0 + values * (1.0 - sigma))


def head_part(tokens, w_head, keep):
    normed_bf = layer_norm(tokens.astype(F32))[0].astype(BF)
    preact = jnp.dot(normed_bf, w_head, preferred_element_type=F32)
    hidden = jax.nn.silu(preact).astype(BF)
    gate = hidden[:, :HEAD_DIM]
    values = hidden[:, HEAD_DIM : 2 * HEAD_DIM].reshape(HEADS, ROWS, HEAD_DIM)
    queries = hidden[:, 2 * HEAD_DIM : 3 * HEAD_DIM].reshape(HEADS, ROWS, HEAD_DIM)
    keys = hidden[:, 3 * HEAD_DIM :].reshape(HEADS, ROWS, HEAD_DIM)
    scores = jnp.einsum("bid,bjd->bij", queries, keys, preferred_element_type=F32) * HEAD_DIM**-0.5
    attn = jnp.where(keep, jax.nn.silu(scores) * (1.0 / LMAX), 0.0).astype(BF)
    mixed = jnp.einsum("bij,bjd->bid", attn, values, preferred_element_type=F32).reshape(
        HEADS * ROWS, HEAD_DIM
    )
    mean = jnp.mean(mixed, axis=-1)
    center = mixed - mean[:, None]
    spread = jnp.sum(center * center, axis=-1)
    return normed_bf, preact, gate, values, queries, keys, scores, attn, center, mean, spread


def per_device(acts_fwd, acts_bwd, cotangent, lens_fwd, lens_bwd, w_proj, w_out):
    loss_scale = 1.0 / math.sqrt(48 * ROWS)

    mine = jnp.concatenate(
        [
            w_proj[0].reshape(16, 4, HEADS, HEAD_DIM).transpose(2, 0, 1, 3).reshape(HEADS, 16, 512),
            w_out[0].T.reshape(16, HEADS, HEAD_DIM).transpose(1, 0, 2),
        ],
        axis=-1,
    ).astype(BF)
    group = exchanged(mine).reshape(64, 640)
    weights = lax.all_gather(group, ALONG_Z, axis=0, tiled=True)
    w_head = weights[:, :512]
    w_back = weights[:, 512:]

    lens = jnp.stack([lens_fwd[0, 0], lens_bwd[0, 0]]).reshape(1, 8).astype(BF)
    pack = jnp.concatenate(
        [acts_fwd[0], acts_bwd[0], cotangent[0], jnp.pad(lens, ((0, 15), (0, 760)))], axis=0
    )
    by_core = shifted(after(pack, mine), "c", 1)
    late = after(pack, group)
    by_chip = shifted(late, "x", 1)
    by_both = lax.ppermute(late, QUAD, [(i, 3 - i) for i in range(4)])
    xi, ci = lax.axis_index("x"), lax.axis_index("c")
    both = jnp.stack([jnp.stack([pack, by_core]), jnp.stack([by_chip, by_both])])
    both = jnp.where(xi == 0, both, both[::-1])
    both = jnp.where(ci == 0, both, both[:, ::-1])
    blocks = both.reshape(4, 400, 768)
    tok_f = blocks[:, :128].reshape(512, 768)
    tok_b = blocks[:, 128:256].reshape(512, 768)
    cotan = blocks[:, 256:384].reshape(512, 768)
    all_lens = blocks[:, 384, :8].astype(jnp.int32)
    keep_f = jagged_mask(all_lens[:, :4])
    keep_b = jagged_mask(all_lens[:, 4:])

    _, _, gate_f, _, _, _, _, _, center_f, mean_f, spread_f = head_part(tok_f, w_head, keep_f)
    normed_bf, preact, gate, values, queries, keys, scores, attn, center, mean, spread = head_part(
        tok_b, w_head, keep_b
    )
    grad_y = jnp.dot(cotan, w_back, preferred_element_type=F32)
    grad_mn = grad_y * gate.astype(F32)
    sum_g = jnp.sum(grad_mn, axis=-1)
    sum_gc = jnp.sum(grad_mn * center, axis=-1)

    stats = lax.all_gather(
        jnp.stack([mean_f, spread_f, mean, spread, sum_g, sum_gc]), QUAD, axis=0, tiled=False
    )
    whole_f = jnp.mean(stats[:, 0], axis=0)
    var_f = (
        jnp.sum(stats[:, 1], axis=0)
        + HEAD_DIM * jnp.sum((stats[:, 0] - whole_f) ** 2, axis=0)
    ) * (1.0 / HID)
    inverse_f = lax.rsqrt(var_f + EPS)
    whole = jnp.mean(stats[:, 2], axis=0)
    var = (
        jnp.sum(stats[:, 3], axis=0) + HEAD_DIM * jnp.sum((stats[:, 2] - whole) ** 2, axis=0)
    ) * (1.0 / HID)
    inverse_o = lax.rsqrt(var + EPS)
    mean_g = jnp.sum(stats[:, 4], axis=0) * (1.0 / HID)
    mean_gm = (
        inverse_o
        * jnp.sum(stats[:, 5] + (stats[:, 2] - whole) * stats[:, 4], axis=0)
        * (1.0 / HID)
    )

    gated_f = ((center_f + (mean_f - whole_f)[:, None]) * inverse_f[:, None] * gate_f.astype(F32)).astype(BF)
    part_f = lax.dot_general(
        gated_f, w_back, (((1,), (1,)), ((), ())), preferred_element_type=F32
    ).astype(BF)

    mixed_n = (center + (mean - whole)[:, None]) * inverse_o[:, None]
    gated = (mixed_n * gate.astype(F32)).astype(BF)
    grad_u = grad_y * mixed_n
    grad_mixed = (
        (inverse_o[:, None] * (grad_mn - mean_g[:, None] - mixed_n * mean_gm[:, None]))
        .astype(BF)
        .reshape(HEADS, ROWS, HEAD_DIM)
    )
    grad_mixed = after(grad_mixed, part_f)
    grad_attn = jnp.einsum("bid,bjd->bij", grad_mixed, values, preferred_element_type=F32)
    grad_vals = jnp.einsum("bij,bid->bjd", attn, grad_mixed, preferred_element_type=F32)
    grad_scores = jnp.where(
        keep_b, grad_attn * (1.0 / LMAX) * silu_slope(scores) * HEAD_DIM**-0.5, 0.0
    ).astype(BF)
    grad_q = jnp.einsum("bij,bjd->bid", grad_scores, keys, preferred_element_type=F32)
    grad_k = jnp.einsum("bij,bid->bjd", grad_scores, queries, preferred_element_type=F32)
    flat = (HEADS * ROWS, HEAD_DIM)
    grad_hidden = jnp.concatenate(
        [grad_u, grad_vals.reshape(flat), grad_q.reshape(flat), grad_k.reshape(flat)], axis=1
    )
    grad_pre = (grad_hidden * silu_slope(preact)).astype(BF)

    across = (((0,), (0,)), ((), ()))
    term_proj = lax.dot_general(normed_bf, grad_pre, across, preferred_element_type=F32)
    term_out = lax.dot_general(cotan, gated, across, preferred_element_type=F32)
    term = jnp.concatenate([term_proj, term_out], axis=1) * loss_scale
    part_b = lax.dot_general(
        grad_pre, w_head, (((1,), (1,)), ((), ())), preferred_element_type=F32
    ).astype(BF)

    summed_f = quad_summed(part_f)
    result = (acts_fwd[0].astype(F32) + summed_f).astype(BF)

    zl = lax.axis_index("zl")
    term = term.reshape(Z_HIGH, Z_LOW, 64, 640).transpose(1, 0, 2, 3).astype(BF)
    ahead = shifted(lax.dynamic_index_in_dim(term, (zl + 1) % 3, 0, False), ALONG_Z, 1)
    behind = shifted(lax.dynamic_index_in_dim(term, (zl + 2) % 3, 0, False), ALONG_Z, -1)
    near = lax.dynamic_index_in_dim(term, zl, 0, False).astype(F32)
    near = (near + ahead.astype(F32) + behind.astype(F32)).astype(BF)
    far = exchanged(after(near, result), "zh")
    grad_norm = quad_summed(part_b)
    next_acts = shifted(result, "pipe", 1)
    normed, inverse = layer_norm(acts_bwd[0].astype(F32))
    grad_in = (
        cotangent[0].astype(F32)
        + inverse
        * (
            grad_norm
            - jnp.mean(grad_norm, axis=-1, keepdims=True)
            - normed * jnp.mean(grad_norm * normed, axis=-1, keepdims=True)
        )
    ).astype(BF)
    prev_grads = shifted(grad_in, "pipe", -1)
    total = jnp.sum(far.astype(F32), axis=0)
    final = exchanged(after(total.reshape(HEADS, 16, 640), grad_in, next_acts))
    grad_proj = (
        final[:, :, :512].reshape(HEADS, 16, 4, HEAD_DIM).transpose(1, 2, 0, 3).reshape(16, 4 * HID)
    )
    grad_out = final[:, :, 512:].transpose(1, 0, 2).reshape(16, HID).T
    return next_acts[None], prev_grads[None], grad_proj[None], grad_out[None]


def solution(mesh):
    pipe = mesh.shape["pipe"]
    fine = Mesh(
        mesh.devices.reshape(Z_HIGH, Z_LOW, 2, 2, pipe), ("zh", "zl", "x", "c", "pipe")
    )
    dp = ("zh", "zl", "x", "c")
    rows = P("pipe", dp, None)
    return jax.shard_map(
        per_device,
        mesh=fine,
        in_specs=(rows, rows, rows, rows, rows, rows, P("pipe", None, dp)),
        out_specs=(rows, rows, rows, P("pipe", None, dp)),
        check_vma=False,
    )
```

time: 496 us -> 153 us (0.31)
  the two profiles are of different devices: /device:TPU:24 before, /device:TPU:156 now
where the time goes in v1:
time: 153 us; the launch traced here: 152 us
  starting transfers between devices  43.3 us (28%)
  blocking collectives  41.7 us (27%)
  waiting for transfers between devices  28.8 us (19%)
  other arithmetic  18.7 us (12%)
  matrix products  9.77 us (6%)
  local copies, waits for them, and re-layouts  8.73 us (6%)
    all_gather x1, blocking collectives, per_device(): weights = lax.all_gather(group, ALONG_Z, axis=0, tiled=True)  36.4 us
    ppermute x10, starting transfers between devices, shifted(): lax.ppermute(array, axis, [(i, (i + by) % count) for i in range(count)])  26.7 us
    all_to_all x3, waiting for transfers between devices, exchanged(): return lax.all_to_all(array, axis, split_axis=0, concat_axis=0, tiled=True)  21.5 us
    all_to_all x3, starting transfers between devices, exchanged(): return lax.all_to_all(array, axis, split_axis=0, concat_axis=0, tiled=True)  13 us
    ppermute x10, waiting for transfers between devices, shifted(): lax.ppermute(array, axis, [(i, (i + by) % count) for i in range(count)])  7.22 us
    all_gather x1, blocking collectives, per_device(): lax.all_gather(jnp.stack([mean_f, spread_f, mean, spread, sum_g, sum_gc])...  5.37 us
    ppermute x1, starting transfers between devices, per_device(): by_both = lax.ppermute(late, QUAD, [(i, 3 - i) for i in range(4)])  3.54 us
    unnamed x42, local copies, waits for them, and re-layouts  3.47 us
  transfers between devices with their start and end apart: 14, of which 5 were waited for; matrix products, arithmetic and copies ran while one was open for 5% of the time, Pallas kernels for 0%

profile of v1, /device:TPU:156, one launch (start us, length us, event | category | flops | bytes accessed | tf_op | source)
XLA Modules:
  0.0 152.4 jit_solution(3965428370675960401)
XLA Ops:
  3.2 3.3 %all-to-all-start = ((bf16[4,16,640]{2,1,0:T(8,128)(2,1)}), bf16[4,16,640]{2,1,0:T(8,128)(2,1)S(1)}, u32[]{:S(2)}, u32[]{:S(2)}) async-start(bf16[4,16,640]{2,1,0:T(8,128)(2,1)} %pad_maximum_fusion.1), calls=%async_computation | async-start | bytes 163840 | tf_op jit(solution)/shard_map/all_to_all | solution.py:28
  8.4 2.4 %collective-permute-start = (bf16[400,768]{1,0:T(8,128)(2,1)S(1)}, bf16[400,768]{1,0:T(8,128)(2,1)S(1)}, u32[]{:S(2)}, u32[]{:S(2)}) collective-permute-start(bf16[400,768]{1,0:T(8,128)(2,1)S(1)} %fusion.11), channel_id=1, source_target_pairs={{0,16},{16,0},{1,17},{17,1},{2,18},{18,2},{3,19},{19,3},{4,20},{20... | collective-permute-start | bytes 1843208 | tf_op jit(solution)/shard_map/ppermute | solution.py:24
  11.2 3.5 %collective-permute-start.2 = (bf16[400,768]{1,0:T(8,128)(2,1)S(1)}, bf16[400,768]{1,0:T(8,128)(2,1)S(1)}, u32[]{:S(2)}, u32[]{:S(2)}) collective-permute-start(bf16[400,768]{1,0:T(8,128)(2,1)S(1)} %fusion.11), channel_id=1, source_target_pairs={{0,48},{16,32},{32,16},{48,0},{1,49},{17,33},{33,17},{49,1},{2,50}... | collective-permute-start | bytes 1843208 | tf_op jit(solution)/shard_map/ppermute | solution.py:107
  14.8 2.0 %collective-permute-start.1 = (bf16[400,768]{1,0:T(8,128)(2,1)S(1)}, bf16[400,768]{1,0:T(8,128)(2,1)}, u32[]{:S(2)}, u32[]{:S(2)}) collective-permute-start(bf16[400,768]{1,0:T(8,128)(2,1)S(1)} %fusion.11), channel_id=1, source_target_pairs={{0,32},{32,0},{1,33},{33,1},{2,34},{34,2},{3,35},{35,3},{4,36},{36... | collective-permute-start | bytes 1843208 | tf_op jit(solution)/shard_map/ppermute | solution.py:24
  16.8 36.4 %all_gather.9 = bf16[768,640]{1,0:T(8,128)(2,1)} all-gather(bf16[64,640]{1,0:T(8,128)(2,1)S(1)} %bitcast.250), channel_id=1, replica_groups=mesh['zh'=4,'zl'=3,'x'=2,'c'=2,'pipe'=16] {'zh','zl'}, dimensions={0}, use_global_device_ids=true | all-gather | bytes 1064960 | tf_op jit(solution)/shard_map/all_gather | solution.py:96
  56.0 2.0 %fusion.74 = (bf16[4,128,768]{2,1,0:T(8,128)(2,1)S(1)}, f32[4,128,768]{2,1,0:T(8,128)}, f32[4,128,768]{2,1,0:T(8,128)}) fusion(bf16[4,400,768]{2,1,0:T(8,128)(2,1)S(1)} %bitcast.218), kind=kLoop, calls=%fused_computation.164 | loop fusion | flops 786432 | bytes 6291456 | tf_op jit(solution)/shard_map/slice | solution.py:115
  59.5 1.9 %copy.54 = f32[512,768]{0,1:T(8,128)S(1)} copy(f32[512,768]{1,0:T(8,128)} %bitcast.225) | data formatting | bytes 3145728 | tf_op jit(solution)/shard_map/convert_element_type | solution.py:67
  61.4 1.7 %fusion.2 = bf16[512,768]{1,0:T(8,128)(2,1)S(1)} fusion(f32[4,128,768]{2,1,0:T(8,128)} %get-tuple-element.31, f32[512]{0:T(512)S(1)} %rsqrt_bitcast_fusion.1, f32[512]{0:T(512)S(1)} %get-tuple-element.59), kind=kLoop, calls=%fused_computation.7 | loop fusion | flops 1179648 | bytes 2363392 | tf_op jit(solution)/shard_map/convert_element_type | solution.py:67
  72.7 5.4 %all-gather.1 = f32[4,6,512]{2,1,0:T(8,128)S(1)} all-gather(f32[1,6,512]{2,1,0:T(8,128)S(1)} %bitcast.257), channel_id=2, replica_groups=mesh['zh'=4,'zl'=3,'x'=2,'c'=2,'pipe'=16] {'x','c'}, dimensions={0}, use_global_device_ids=true | all-gather | bytes 61440 | tf_op jit(solution)/shard_map/all_gather | solution.py:129
  83.2 3.7 %collective-permute-start.3 = (bf16[2,128,768]{2,1,0:T(8,128)(2,1)S(1)}, bf16[2,128,768]{2,1,0:T(8,128)(2,1)S(1)}, u32[]{:S(2)}, u32[]{:S(2)}) collective-permute-start(bf16[2,128,768]{2,1,0:T(8,128)(2,1)S(1)} %dynamic-slice_bitcast_fusion.1), channel_id=1, source_target_pairs={{0,32},{32,0},{1,33},{33,1},{2,34},{34,2},{3,35},{35,3},{4,36},{36... | collective-permute-start | bytes 1179656 | tf_op jit(solution)/shard_map/ppermute | solution.py:24
  89.3 1.9 %collective-permute-start.9 = (bf16[4,64,640]{2,1,0:T(8,128)(2,1)S(1)}, bf16[4,64,640]{2,1,0:T(8,128)(2,1)S(1)}, u32[]{:S(2)}, u32[]{:S(2)}) collective-permute-start(bf16[4,64,640]{2,1,0:T(8,128)(2,1)S(1)} %get-tuple-element.32), channel_id=1, source_target_pairs={{0,64},{64,128},{128,192},{192,256},{256,320},{320,384},{384,448},... | collective-permute-start | bytes 983048 | tf_op jit(solution)/shard_map/ppermute | solution.py:24
  91.2 3.9 %collective-permute-start.10 = (bf16[4,64,640]{2,1,0:T(8,128)(2,1)S(1)}, bf16[4,64,640]{2,1,0:T(8,128)(2,1)S(1)}, u32[]{:S(2)}, u32[]{:S(2)}) collective-permute-start(bf16[4,64,640]{2,1,0:T(8,128)(2,1)S(1)} %get-tuple-element.33), channel_id=1, source_target_pairs={{0,704},{64,0},{128,64},{192,128},{256,192},{320,256},{384,320},{4... | collective-permute-start | bytes 983048 | tf_op jit(solution)/shard_map/ppermute | solution.py:24
  95.8 2.2 %collective-permute-start.6 = (bf16[2,128,768]{2,1,0:T(8,128)(2,1)S(1)}, bf16[2,128,768]{2,1,0:T(8,128)(2,1)S(1)}, u32[]{:S(2)}, u32[]{:S(2)}) collective-permute-start(bf16[2,128,768]{2,1,0:T(8,128)(2,1)S(1)} %dynamic-slice_bitcast_fusion), channel_id=1, source_target_pairs={{0,32},{32,0},{1,33},{33,1},{2,34},{34,2},{3,35},{35,3},{4,36},{36... | collective-permute-start | bytes 1179656 | tf_op jit(solution)/shard_map/ppermute | solution.py:24
  98.0 2.9 %collective-permute-done.9 = bf16[4,64,640]{2,1,0:T(8,128)(2,1)S(1)} collective-permute-done((bf16[4,64,640]{2,1,0:T(8,128)(2,1)S(1)}, bf16[4,64,640]{2,1,0:T(8,128)(2,1)S(1)}, u32[]{:S(2)}, u32[]{:S(2)}) %collective-permute-start.9) | collective-permute-done | bytes 327712 | tf_op jit(solution)/shard_map/ppermute | solution.py:24
  100.9 2.4 %collective-permute-done.10 = bf16[4,64,640]{2,1,0:T(8,128)(2,1)S(1)} collective-permute-done((bf16[4,64,640]{2,1,0:T(8,128)(2,1)S(1)}, bf16[4,64,640]{2,1,0:T(8,128)(2,1)S(1)}, u32[]{:S(2)}, u32[]{:S(2)}) %collective-permute-start.10) | collective-permute-done | bytes 327712 | tf_op jit(solution)/shard_map/ppermute | solution.py:24
  104.3 2.1 %collective-permute-start.4 = (bf16[128,768]{1,0:T(8,128)(2,1)S(1)}, bf16[128,768]{1,0:T(8,128)(2,1)S(1)}, u32[]{:S(2)}, u32[]{:S(2)}) collective-permute-start(bf16[128,768]{1,0:T(8,128)(2,1)S(1)} %fusion.43), channel_id=1, source_target_pairs={{0,16},{16,0},{1,17},{17,1},{2,18},{18,2},{3,19},{19,3},{4,20},{20... | collective-permute-start | bytes 589832 | tf_op jit(solution)/shard_map/ppermute | solution.py:24
  106.3 1.9 %collective-permute-done.6 = bf16[2,128,768]{2,1,0:T(8,128)(2,1)S(1)} collective-permute-done((bf16[2,128,768]{2,1,0:T(8,128)(2,1)S(1)}, bf16[2,128,768]{2,1,0:T(8,128)(2,1)S(1)}, u32[]{:S(2)}, u32[]{:S(2)}) %collective-permute-start.6) | collective-permute-done | bytes 393248 | tf_op jit(solution)/shard_map/ppermute | solution.py:24
  108.4 2.1 %collective-permute-start.7 = (bf16[128,768]{1,0:T(8,128)(2,1)S(1)}, bf16[128,768]{1,0:T(8,128)(2,1)S(1)}, u32[]{:S(2)}, u32[]{:S(2)}) collective-permute-start(bf16[128,768]{1,0:T(8,128)(2,1)S(1)} %fusion.44), channel_id=1, source_target_pairs={{0,16},{16,0},{1,17},{17,1},{2,18},{18,2},{3,19},{19,3},{4,20},{20... | collective-permute-start | bytes 589832 | tf_op jit(solution)/shard_map/ppermute | solution.py:24
  110.5 4.7 %collective-permute-start.5 = (bf16[128,768]{1,0:T(8,128)(2,1)S(1)}, bf16[128,768]{1,0:T(8,128)(2,1)S(1)}, u32[]{:S(2)}, u32[]{:S(2)}) collective-permute-start(bf16[128,768]{1,0:T(8,128)(2,1)S(1)} %fusion.34), channel_id=1, source_target_pairs={{0,1},{1,2},{2,3},{3,4},{4,5},{5,6},{6,7},{7,8},{8,9},{9,10},{10,1... | collective-permute-start | bytes 589832 | tf_op jit(solution)/shard_map/ppermute | solution.py:24
  115.3 6.3 %all-to-all-start.1 = ((bf16[4,64,640]{2,1,0:T(8,128)(2,1)}), bf16[4,64,640]{2,1,0:T(8,128)(2,1)S(1)}, u32[]{:S(2)}, u32[]{:S(2)}) async-start(bf16[4,64,640]{2,1,0:T(8,128)(2,1)} %fusion.10), calls=%async_computation.1 | async-start | bytes 655360 | tf_op jit(solution)/shard_map/all_to_all | solution.py:28
  122.0 1.9 %collective-permute-start.8 = (bf16[128,768]{1,0:T(8,128)(2,1)S(1)}, bf16[128,768]{1,0:T(8,128)(2,1)S(1)}, u32[]{:S(2)}, u32[]{:S(2)}) collective-permute-start(bf16[128,768]{1,0:T(8,128)(2,1)S(1)} %fusion.31), channel_id=1, source_target_pairs={{0,15},{1,0},{2,1},{3,2},{4,3},{5,4},{6,5},{7,6},{8,7},{9,8},{10,9... | collective-permute-start | bytes 589832 | tf_op jit(solution)/shard_map/ppermute | solution.py:24
  124.0 16.6 %all-to-all-done.1 = bf16[4,64,640]{2,1,0:T(8,128)(2,1)S(1)} async-done(((bf16[4,64,640]{2,1,0:T(8,128)(2,1)}), bf16[4,64,640]{2,1,0:T(8,128)(2,1)S(1)}, u32[]{:S(2)}, u32[]{:S(2)}) %all-to-all-start.1) | async-done | bytes 327712 | tf_op jit(solution)/shard_map/all_to_all | solution.py:28
  141.3 3.3 %all-to-all-start.2 = ((f32[4,16,640]{2,1,0:T(8,128)}), f32[4,16,640]{2,1,0:T(8,128)S(1)}, u32[]{:S(2)}, u32[]{:S(2)}) async-start(f32[4,16,640]{2,1,0:T(8,128)} %bitcast.72), calls=%async_computation.2 | async-start | bytes 327680 | tf_op jit(solution)/shard_map/all_to_all | solution.py:28
  144.7 4.9 %all-to-all-done.2 = f32[4,16,640]{2,1,0:T(8,128)S(1)} async-done(((f32[4,16,640]{2,1,0:T(8,128)}), f32[4,16,640]{2,1,0:T(8,128)S(1)}, u32[]{:S(2)}, u32[]{:S(2)}) %all-to-all-start.2) | async-done | bytes 163872 | tf_op jit(solution)/shard_map/all_to_all | solution.py:28
  (140 shorter events, 31.7 us)
Async XLA Ops:
  0.6 10.1 %copy-start = (bf16[1,128,768]{2,1,0:T(8,128)(2,1)S(1)}, bf16[1,128,768]{2,1,0:T(8,128)(2,1)}, u32[]{:S(2)}) copy-start(bf16[1,128,768]{2,1,0:T(8,128)(2,1)} %param.8) | copy-start | bytes 589828
  0.6 10.5 %copy-start.8 = (bf16[1,128,768]{2,1,0:T(8,128)(2,1)S(1)}, bf16[1,128,768]{2,1,0:T(8,128)(2,1)}, u32[]{:S(2)}) copy-start(bf16[1,128,768]{2,1,0:T(8,128)(2,1)} %param.9) | copy-start | bytes 589828
  0.7 10.5 %copy-start.6 = (bf16[1,128,768]{2,1,0:T(8,128)(2,1)S(1)}, bf16[1,128,768]{2,1,0:T(8,128)(2,1)}, u32[]{:S(2)}) copy-start(bf16[1,128,768]{2,1,0:T(8,128)(2,1)} %param.7) | copy-start | bytes 589828
  3.2 8.0 %all-to-all-start = ((bf16[4,16,640]{2,1,0:T(8,128)(2,1)}), bf16[4,16,640]{2,1,0:T(8,128)(2,1)S(1)}, u32[]{:S(2)}, u32[]{:S(2)}) async-start(bf16[4,16,640]{2,1,0:T(8,128)(2,1)} %pad_maximum_fusion.1), calls=%async_computation | async-start | bytes 163840 | tf_op jit(solution)/shard_map/all_to_all | solution.py:28
  8.4 44.8 %collective-permute-start = (bf16[400,768]{1,0:T(8,128)(2,1)S(1)}, bf16[400,768]{1,0:T(8,128)(2,1)S(1)}, u32[]{:S(2)}, u32[]{:S(2)}) collective-permute-start(bf16[400,768]{1,0:T(8,128)(2,1)S(1)} %fusion.11), channel_id=1, source_target_pairs={{0,16},{16,0},{1,17},{17,1},{2,18},{18,2},{3,19},{19,3},{4,20},{20... | collective-permute-start | bytes 1843208 | tf_op jit(solution)/shard_map/ppermute | solution.py:24
  11.2 42.1 %collective-permute-start.2 = (bf16[400,768]{1,0:T(8,128)(2,1)S(1)}, bf16[400,768]{1,0:T(8,128)(2,1)S(1)}, u32[]{:S(2)}, u32[]{:S(2)}) collective-permute-start(bf16[400,768]{1,0:T(8,128)(2,1)S(1)} %fusion.11), channel_id=1, source_target_pairs={{0,48},{16,32},{32,16},{48,0},{1,49},{17,33},{33,17},{49,1},{2,50}... | collective-permute-start | bytes 1843208 | tf_op jit(solution)/shard_map/ppermute | solution.py:107
  14.8 38.5 %collective-permute-start.1 = (bf16[400,768]{1,0:T(8,128)(2,1)S(1)}, bf16[400,768]{1,0:T(8,128)(2,1)}, u32[]{:S(2)}, u32[]{:S(2)}) collective-permute-start(bf16[400,768]{1,0:T(8,128)(2,1)S(1)} %fusion.11), channel_id=1, source_target_pairs={{0,32},{32,0},{1,33},{33,1},{2,34},{34,2},{3,35},{35,3},{4,36},{36... | collective-permute-start | bytes 1843208 | tf_op jit(solution)/shard_map/ppermute | solution.py:24
  72.6 9.5 %copy-start.18 = (bf16[4,128,128]{2,1,0:T(8,128)(2,1)S(1)}, bf16[4,128,128]{2,1,0:T(8,128)(2,1)}, u32[]{:S(2)}) copy-start(bf16[4,128,128]{2,1,0:T(8,128)(2,1)} %copy-done.17) | copy-start | bytes 393220
  79.4 3.0 %copy-start.16 = (bf16[512,128]{1,0:T(8,128)(2,1)S(1)}, bf16[512,128]{1,0:T(8,128)(2,1)}, u32[]{:S(2)}) copy-start(bf16[512,128]{1,0:T(8,128)(2,1)} %copy-done.15) | copy-start | bytes 393220
  79.4 3.0 %copy-start.19 = (f32[4,128,128]{2,1,0:T(8,128)S(1)}, f32[4,128,128]{2,1,0:T(8,128)}, u32[]{:S(2)}) copy-start(f32[4,128,128]{2,1,0:T(8,128)} %get-tuple-element.66) | copy-start | bytes 786436
  82.7 4.5 %copy-start.10 = (f32[512,512]{1,0:T(8,128)S(1)}, f32[512,512]{1,0:T(8,128)}, u32[]{:S(2)}) copy-start(f32[512,512]{1,0:T(8,128)} %get-tuple-element.64) | copy-start | bytes 3145732
  83.2 20.9 %collective-permute-start.3 = (bf16[2,128,768]{2,1,0:T(8,128)(2,1)S(1)}, bf16[2,128,768]{2,1,0:T(8,128)(2,1)S(1)}, u32[]{:S(2)}, u32[]{:S(2)}) collective-permute-start(bf16[2,128,768]{2,1,0:T(8,128)(2,1)S(1)} %dynamic-slice_bitcast_fusion.1), channel_id=1, source_target_pairs={{0,32},{32,0},{1,33},{33,1},{2,34},{34,2},{3,35},{35,3},{4,36},{36... | collective-permute-start | bytes 1179656 | tf_op jit(solution)/shard_map/ppermute | solution.py:24
  89.0 6.2 %copy-start.5 = (bf16[768,640]{1,0:T(8,128)(2,1)S(1)}, bf16[768,640]{1,0:T(8,128)(2,1)}, u32[]{:S(2)}) copy-start(bf16[768,640]{1,0:T(8,128)(2,1)} %all_gather.9) | copy-start | bytes 2949124
  89.3 11.6 %collective-permute-start.9 = (bf16[4,64,640]{2,1,0:T(8,128)(2,1)S(1)}, bf16[4,64,640]{2,1,0:T(8,128)(2,1)S(1)}, u32[]{:S(2)}, u32[]{:S(2)}) collective-permute-start(bf16[4,64,640]{2,1,0:T(8,128)(2,1)S(1)} %get-tuple-element.32), channel_id=1, source_target_pairs={{0,64},{64,128},{128,192},{192,256},{256,320},{320,384},{384,448},... | collective-permute-start | bytes 983048 | tf_op jit(solution)/shard_map/ppermute | solution.py:24
  91.2 12.0 %collective-permute-start.10 = (bf16[4,64,640]{2,1,0:T(8,128)(2,1)S(1)}, bf16[4,64,640]{2,1,0:T(8,128)(2,1)S(1)}, u32[]{:S(2)}, u32[]{:S(2)}) collective-permute-start(bf16[4,64,640]{2,1,0:T(8,128)(2,1)S(1)} %get-tuple-element.33), channel_id=1, source_target_pairs={{0,704},{64,0},{128,64},{192,128},{256,192},{320,256},{384,320},{4... | collective-permute-start | bytes 983048 | tf_op jit(solution)/shard_map/ppermute | solution.py:24
  95.8 12.4 %collective-permute-start.6 = (bf16[2,128,768]{2,1,0:T(8,128)(2,1)S(1)}, bf16[2,128,768]{2,1,0:T(8,128)(2,1)S(1)}, u32[]{:S(2)}, u32[]{:S(2)}) collective-permute-start(bf16[2,128,768]{2,1,0:T(8,128)(2,1)S(1)} %dynamic-slice_bitcast_fusion), channel_id=1, source_target_pairs={{0,32},{32,0},{1,33},{33,1},{2,34},{34,2},{3,35},{35,3},{4,36},{36... | collective-permute-start | bytes 1179656 | tf_op jit(solution)/shard_map/ppermute | solution.py:24
  104.2 6.3 %copy-start.7 = (bf16[1,128,768]{2,1,0:T(8,128)(2,1)S(1)}, bf16[1,128,768]{2,1,0:T(8,128)(2,1)}, u32[]{:S(2)}) copy-start(bf16[1,128,768]{2,1,0:T(8,128)(2,1)} %param.7) | copy-start | bytes 589828
  104.3 6.2 %collective-permute-start.4 = (bf16[128,768]{1,0:T(8,128)(2,1)S(1)}, bf16[128,768]{1,0:T(8,128)(2,1)S(1)}, u32[]{:S(2)}, u32[]{:S(2)}) collective-permute-start(bf16[128,768]{1,0:T(8,128)(2,1)S(1)} %fusion.43), channel_id=1, source_target_pairs={{0,16},{16,0},{1,17},{17,1},{2,18},{18,2},{3,19},{19,3},{4,20},{20... | collective-permute-start | bytes 589832 | tf_op jit(solution)/shard_map/ppermute | solution.py:24
  108.3 13.5 %copy-start.9 = (bf16[1,128,768]{2,1,0:T(8,128)(2,1)S(1)}, bf16[1,128,768]{2,1,0:T(8,128)(2,1)}, u32[]{:S(2)}) copy-start(bf16[1,128,768]{2,1,0:T(8,128)(2,1)} %param.9) | copy-start | bytes 589828
  108.4 13.2 %collective-permute-start.7 = (bf16[128,768]{1,0:T(8,128)(2,1)S(1)}, bf16[128,768]{1,0:T(8,128)(2,1)S(1)}, u32[]{:S(2)}, u32[]{:S(2)}) collective-permute-start(bf16[128,768]{1,0:T(8,128)(2,1)S(1)} %fusion.44), channel_id=1, source_target_pairs={{0,16},{16,0},{1,17},{17,1},{2,18},{18,2},{3,19},{19,3},{4,20},{20... | collective-permute-start | bytes 589832 | tf_op jit(solution)/shard_map/ppermute | solution.py:24
  110.5 30.8 %collective-permute-start.5 = (bf16[128,768]{1,0:T(8,128)(2,1)S(1)}, bf16[128,768]{1,0:T(8,128)(2,1)S(1)}, u32[]{:S(2)}, u32[]{:S(2)}) collective-permute-start(bf16[128,768]{1,0:T(8,128)(2,1)S(1)} %fusion.34), channel_id=1, source_target_pairs={{0,1},{1,2},{2,3},{3,4},{4,5},{5,6},{6,7},{7,8},{8,9},{9,10},{10,1... | collective-permute-start | bytes 589832 | tf_op jit(solution)/shard_map/ppermute | solution.py:24
  115.3 25.3 %all-to-all-start.1 = ((bf16[4,64,640]{2,1,0:T(8,128)(2,1)}), bf16[4,64,640]{2,1,0:T(8,128)(2,1)S(1)}, u32[]{:S(2)}, u32[]{:S(2)}) async-start(bf16[4,64,640]{2,1,0:T(8,128)(2,1)} %fusion.10), calls=%async_computation.1 | async-start | bytes 655360 | tf_op jit(solution)/shard_map/all_to_all | solution.py:28
  122.0 22.6 %collective-permute-start.8 = (bf16[128,768]{1,0:T(8,128)(2,1)S(1)}, bf16[128,768]{1,0:T(8,128)(2,1)S(1)}, u32[]{:S(2)}, u32[]{:S(2)}) collective-permute-start(bf16[128,768]{1,0:T(8,128)(2,1)S(1)} %fusion.31), channel_id=1, source_target_pairs={{0,15},{1,0},{2,1},{3,2},{4,3},{5,4},{6,5},{7,6},{8,7},{9,8},{10,9... | collective-permute-start | bytes 589832 | tf_op jit(solution)/shard_map/ppermute | solution.py:24
  141.3 8.3 %all-to-all-start.2 = ((f32[4,16,640]{2,1,0:T(8,128)}), f32[4,16,640]{2,1,0:T(8,128)S(1)}, u32[]{:S(2)}, u32[]{:S(2)}) async-start(f32[4,16,640]{2,1,0:T(8,128)} %bitcast.72), calls=%async_computation.2 | async-start | bytes 327680 | tf_op jit(solution)/shard_map/all_to_all | solution.py:28
  (10 other events, 14.2 us)

commit v2 on v1

v2 whole, which is shorter than its diff:
```python
import math

import jax
import jax.numpy as jnp
from jax import lax
from jax.experimental import pallas as pl
from jax.experimental.pallas import tpu as pltpu
from jax.sharding import Mesh
from jax.sharding import PartitionSpec as P


HEADS = 4
HEAD_DIM = 128
HID = 512
LMAX = 64
EPS = 1e-05
Z_HIGH, Z_LOW = 4, 3
QUAD = ("x", "c")
ALONG_Z = ("zh", "zl")
ROWS = 128
BF = jnp.bfloat16
F32 = jnp.float32


def shifted(array, axis, by):
    count = lax.axis_size(axis)
    return lax.ppermute(array, axis, [(i, (i + by) % count) for i in range(count)])


def exchanged(array, axis=QUAD):
    return lax.all_to_all(array, axis, split_axis=0, concat_axis=0, tiled=True)


def after(array, *others):
    return lax.optimization_barrier((array, *others))[0]


def quad_summed(parts):
    parts = parts.reshape(2, 2, 2, ROWS, 768)
    arrived = shifted(parts[:, :, 1], "c", 1)
    pair = parts[:, :, 0].astype(F32) + arrived.astype(F32)
    arrived = shifted(pair[:, 1].astype(BF), "x", 1)
    return pair[:, 0] + arrived.astype(F32)


def layer_norm(values):
    center = values - jnp.mean(values, axis=-1, keepdims=True)
    inverse = lax.rsqrt(jnp.mean(center * center, axis=-1, keepdims=True) + EPS)
    return (center * inverse, inverse)


def contract(left, right, left_dim, right_dim):
    return lax.dot_general(
        left, right, (((left_dim,), (right_dim,)), ((), ())), preferred_element_type=F32
    )


def block(r):
    return slice(r * ROWS, (r + 1) * ROWS)


def jagged_mask(row, first):
    lane = lax.broadcasted_iota(jnp.int32, (1, ROWS), 1)
    i = lax.broadcasted_iota(jnp.int32, (ROWS, ROWS), 0).astype(F32)
    j = lax.broadcasted_iota(jnp.int32, (ROWS, ROWS), 1).astype(F32)
    start = jnp.zeros((ROWS, ROWS), F32)
    for k in range(3):
        inside = (lane >= first) & (lane <= first + k)
        end = jnp.sum(jnp.where(inside, row, 0.0), axis=1, keepdims=True)
        start = jnp.maximum(start, jnp.where(i >= end, end, 0.0))
    return (j >= start) & (j <= i)


def in_columns(columns):
    lane = lax.broadcasted_iota(jnp.int32, (ROWS, ROWS), 1)
    whole = jnp.zeros((ROWS, ROWS), F32)
    for k, column in enumerate(columns):
        whole = jnp.where(lane == k, column, whole)
    return whole.T[:8]


def first_kernel(
    place, own, core, chip, both, weights,
    stats, center_f, gate_f, normed_b, hidden_b, slope_b, attn_b, factor_b, center_b, grad_y,
    normed_f, hidden_f,
):
    sources = (own, core, chip, both)
    w_head = weights[:, :512]
    for r, source in enumerate(sources):
        normed_f[block(r)] = layer_norm(source[:ROWS].astype(F32))[0].astype(BF)
        normed_b[block(r)] = layer_norm(source[ROWS : 2 * ROWS].astype(F32))[0].astype(BF)
    for r in range(4):
        preact = jnp.dot(normed_f[block(r)], w_head, preferred_element_type=F32)
        hidden_f[block(r)] = (preact * jax.nn.sigmoid(preact)).astype(BF)
        preact = jnp.dot(normed_b[block(r)], w_head, preferred_element_type=F32)
        sigma = jax.nn.sigmoid(preact)
        hidden_b[block(r)] = (preact * sigma).astype(BF)
        slope_b[block(r)] = sigma * (1.0 + preact * (1.0 - sigma))
        grad_y[block(r)] = jnp.dot(
            sources[r][2 * ROWS : 3 * ROWS], weights[:, 512:], preferred_element_type=F32
        )
    gate_f[...] = hidden_f[:, :HEAD_DIM]
    for r, source in enumerate(sources):
        row = source[3 * ROWS :, :ROWS].astype(F32)[:1]
        columns = []
        for hidden, center_ref, first in ((hidden_f, center_f, 0), (hidden_b, center_b, 4)):
            values = hidden[block(r), HEAD_DIM : 2 * HEAD_DIM]
            queries = hidden[block(r), 2 * HEAD_DIM : 3 * HEAD_DIM]
            keys = hidden[block(r), 3 * HEAD_DIM :]
            keep = jagged_mask(row, first)
            scores = contract(queries, keys, 1, 1) * HEAD_DIM**-0.5
            sigma = jax.nn.sigmoid(scores)
            attn = jnp.where(keep, scores * sigma * (1.0 / LMAX), 0.0).astype(BF)
            mixed = jnp.dot(attn, values, preferred_element_type=F32)
            mean = jnp.mean(mixed, axis=1, keepdims=True)
            center = mixed - mean
            center_ref[block(r)] = center
            columns += [mean, jnp.sum(center * center, axis=1, keepdims=True)]
            if first:
                attn_b[r] = attn
                factor_b[r] = jnp.where(
                    keep,
                    sigma * (1.0 + scores * (1.0 - sigma)) * (HEAD_DIM**-0.5 / LMAX),
                    0.0,
                )
                grad_mn = grad_y[block(r)] * hidden[block(r), :HEAD_DIM].astype(F32)
                columns += [
                    jnp.sum(grad_mn, axis=1, keepdims=True),
                    jnp.sum(grad_mn * center, axis=1, keepdims=True),
                ]
        stats[place[0] ^ r] = in_columns(columns)


def second_kernel(
    place, stats, own, core, chip, both,
    center_f, gate_f, normed_b, hidden_b, slope_b, attn_b, factor_b, center_b, grad_y,
    term_own, term_up, term_down, gated_f, grad_pre,
    gated_b, term,
):
    own_head = place[0]
    for r in range(4):
        b = own_head ^ r
        mine = stats[own_head, b]
        every = [stats[h, b] for h in range(4)]
        whole = (every[0] + every[1] + every[2] + every[3]) * (1.0 / 4)
        gaps = [one - whole for one in every]
        spread = (gaps[0] ** 2 + gaps[1] ** 2 + gaps[2] ** 2 + gaps[3] ** 2) * HEAD_DIM
        inverse_f = lax.rsqrt((4 * whole[1:2] + spread[0:1]) * (1.0 / HID) + EPS)
        inverse_b = lax.rsqrt((4 * whole[3:4] + spread[2:3]) * (1.0 / HID) + EPS)
        mean_g = 4 * whole[4:5] * (1.0 / HID)
        crossed = 4 * whole[5:6]
        for one, gap in zip(every, gaps):
            crossed = crossed + gap[2:3] * one[4:5]
        mean_gm = inverse_b * crossed * (1.0 / HID)
        lines = [mine[0:1] - whole[0:1], inverse_f, mine[2:3] - whole[2:3], inverse_b, mean_g, mean_gm]
        row = lax.broadcasted_iota(jnp.int32, (ROWS, ROWS), 0)
        table = jnp.zeros((ROWS, ROWS), F32)
        for k, line in enumerate(lines):
            table = jnp.where(row == k, line, table)
        table = table.T
        gap_f, inverse_f, gap_b, inverse_b, mean_g, mean_gm = (table[:, k : k + 1] for k in range(6))

        mixed_n = (center_f[block(r)] + gap_f) * inverse_f
        gated_f[block(r)] = (mixed_n * gate_f[block(r)].astype(F32)).astype(BF)
        gate = hidden_b[block(r), :HEAD_DIM].astype(F32)
        values = hidden_b[block(r), HEAD_DIM : 2 * HEAD_DIM]
        queries = hidden_b[block(r), 2 * HEAD_DIM : 3 * HEAD_DIM]
        keys = hidden_b[block(r), 3 * HEAD_DIM :]
        mixed_n = (center_b[block(r)] + gap_b) * inverse_b
        gated_b[block(r)] = (mixed_n * gate).astype(BF)
        grad = grad_y[block(r)]
        grad_mixed = (inverse_b * (grad * gate - mean_g - mixed_n * mean_gm)).astype(BF)
        grad_vals = contract(attn_b[r], grad_mixed, 0, 0)
        grad_scores = (contract(grad_mixed, values, 1, 1) * factor_b[r]).astype(BF)
        grad_q = jnp.dot(grad_scores, keys, preferred_element_type=F32)
        grad_k = contract(grad_scores, queries, 0, 0)
        for k, part in enumerate((grad * mixed_n, grad_vals, grad_q, grad_k)):
            columns = slice(k * HEAD_DIM, (k + 1) * HEAD_DIM)
            grad_pre[block(r), columns] = (part * slope_b[block(r), columns]).astype(BF)
    loss_scale = 1.0 / math.sqrt(48 * ROWS)
    term[:, :512] = (contract(normed_b[...], grad_pre[...], 0, 0) * loss_scale).astype(BF)
    term_out = sum(
        contract(source[2 * ROWS : 3 * ROWS], gated_b[block(r)], 0, 0)
        for r, source in enumerate((own, core, chip, both))
    )
    term[:, 512:] = (term_out * loss_scale).astype(BF)
    for k, out in enumerate((term_own, term_up, term_down)):
        low = lax.rem(place[1] + k, Z_LOW)
        for high in range(Z_HIGH):
            out[high] = term[pl.ds(pl.multiple_of((high * Z_LOW + low) * 64, 64), 64)]


def called(kernel, shapes, scratch, place, *operands):
    scalar = pl.BlockSpec(memory_space=pltpu.SMEM)
    whole = pl.BlockSpec(memory_space=pltpu.VMEM)
    return pl.pallas_call(
        kernel,
        out_shape=[jax.ShapeDtypeStruct(*shape) for shape in shapes],
        in_specs=[scalar] + [whole] * len(operands),
        out_specs=[whole] * len(shapes),
        scratch_shapes=[pltpu.VMEM(*shape) for shape in scratch],
    )(place, *operands)


def per_device(acts_fwd, acts_bwd, cotangent, lens_fwd, lens_bwd, w_proj, w_out):
    mine = jnp.concatenate(
        [
            w_proj[0].reshape(16, 4, HEADS, HEAD_DIM).transpose(2, 0, 1, 3).reshape(HEADS, 16, 512),
            w_out[0].T.reshape(16, HEADS, HEAD_DIM).transpose(1, 0, 2),
        ],
        axis=-1,
    ).astype(BF)
    group = exchanged(mine).reshape(64, 640)
    weights = lax.all_gather(group, ALONG_Z, axis=0, tiled=True)

    lens = jnp.stack([lens_fwd[0, 0], lens_bwd[0, 0]]).reshape(1, 8).astype(BF)
    pack = jnp.concatenate(
        [acts_fwd[0], acts_bwd[0], cotangent[0], jnp.pad(lens, ((0, 15), (0, 760)))], axis=0
    )
    by_core = shifted(after(pack, mine), "c", 1)
    late = after(pack, group)
    by_chip = shifted(late, "x", 1)
    by_both = lax.ppermute(late, QUAD, [(i, 3 - i) for i in range(4)])
    sources = (pack, by_core, by_chip, by_both)
    place = jnp.stack([lax.axis_index(QUAD), lax.axis_index("zl")]).astype(jnp.int32)

    tall, square = (HEADS * ROWS, HEAD_DIM), (HEADS, ROWS, ROWS)
    stats, *kept = called(
        first_kernel,
        (
            ((HEADS, 8, ROWS), F32),
            (tall, F32),
            (tall, BF),
            ((512, 768), BF),
            ((512, 512), BF),
            ((512, 512), F32),
            (square, BF),
            (square, F32),
            (tall, F32),
            (tall, F32),
        ),
        (((512, 768), BF), ((512, 512), BF)),
        place,
        *sources,
        weights,
    )
    every = lax.all_gather(stats, QUAD, axis=0, tiled=False)
    strided = ((Z_HIGH, 64, 640), BF)
    term_own, term_up, term_down, gated_f, grad_pre = called(
        second_kernel,
        (strided, strided, strided, (tall, BF), ((512, 512), BF)),
        ((tall, BF), ((768, 640), BF)),
        place,
        every,
        *sources,
        *kept,
    )

    ahead = shifted(term_up, ALONG_Z, 1)
    behind = shifted(term_down, ALONG_Z, -1)
    near = (term_own.astype(F32) + ahead.astype(F32) + behind.astype(F32)).astype(BF)
    far = exchanged(near, "zh")

    parts = jnp.stack(
        [
            contract(gated_f, weights[:, 512:], 1, 1).astype(BF),
            contract(grad_pre, weights[:, :512], 1, 1).astype(BF),
        ]
    )
    summed = quad_summed(parts.reshape(2, HEADS, ROWS, 768))
    result = (acts_fwd[0].astype(F32) + summed[0]).astype(BF)
    next_acts = shifted(result, "pipe", 1)
    grad_norm = summed[1]
    normed, inverse = layer_norm(acts_bwd[0].astype(F32))
    grad_in = (
        cotangent[0].astype(F32)
        + inverse
        * (
            grad_norm
            - jnp.mean(grad_norm, axis=-1, keepdims=True)
            - normed * jnp.mean(grad_norm * normed, axis=-1, keepdims=True)
        )
    ).astype(BF)
    prev_grads = shifted(grad_in, "pipe", -1)

    total = jnp.sum(far.astype(F32), axis=0)
    final = exchanged(total.reshape(HEADS, 16, 640))
    grad_proj = (
        final[:, :, :512].reshape(HEADS, 16, 4, HEAD_DIM).transpose(1, 2, 0, 3).reshape(16, 4 * HID)
    )
    grad_out = final[:, :, 512:].transpose(1, 0, 2).reshape(16, HID).T
    return next_acts[None], prev_grads[None], grad_proj[None], grad_out[None]


def solution(mesh):
    pipe = mesh.shape["pipe"]
    fine = Mesh(
        mesh.devices.reshape(Z_HIGH, Z_LOW, 2, 2, pipe), ("zh", "zl", "x", "c", "pipe")
    )
    dp = ("zh", "zl", "x", "c")
    rows = P("pipe", dp, None)
    return jax.shard_map(
        per_device,
        mesh=fine,
        in_specs=(rows, rows, rows, rows, rows, rows, P("pipe", None, dp)),
        out_specs=(rows, rows, rows, P("pipe", None, dp)),
        check_vma=False,
    )
```

time: 153 us -> 145 us (0.948)
  the two profiles are of different devices: /device:TPU:156 before, /device:TPU:56 now
where the time goes in v2:
time: 145 us; the launch traced here: 144 us
  blocking collectives  47.3 us (33%)
  starting transfers between devices  37 us (26%)
  waiting for transfers between devices  29.5 us (20%)
  Pallas kernels  12.4 us (9%)
  other arithmetic  8.67 us (6%)
  local copies, waits for them, and re-layouts  5.87 us (4%)
  matrix products  2.05 us (1%)
    all_gather x1, blocking collectives, per_device(): weights = lax.all_gather(group, ALONG_Z, axis=0, tiled=True)  40.5 us
    ppermute x8, starting transfers between devices, shifted(): lax.ppermute(array, axis, [(i, (i + by) % count) for i in range(count)])  24 us
    ppermute x8, waiting for transfers between devices, shifted(): lax.ppermute(array, axis, [(i, (i + by) % count) for i in range(count)])  15.9 us
    all_to_all x3, waiting for transfers between devices, exchanged(): return lax.all_to_all(array, axis, split_axis=0, concat_axis=0, tiled=True)  13.5 us
    pallas_call x2, Pallas kernels, called(): pl.pallas_call(kernel, out_shape=[jax.ShapeDtypeStruct(*shape) for shape...  12.4 us
    all_to_all x3, starting transfers between devices, exchanged(): return lax.all_to_all(array, axis, split_axis=0, concat_axis=0, tiled=True)  11 us
    all_gather x1, blocking collectives, per_device(): every = lax.all_gather(stats, QUAD, axis=0, tiled=False)  6.8 us
    unnamed x29, local copies, waits for them, and re-layouts  4.18 us
  transfers between devices with their start and end apart: 12, of which 5 were waited for; matrix products, arithmetic and copies ran while one was open for 5% of the time, Pallas kernels for 0%

profile of v2, /device:TPU:56, one launch (start us, length us, event | category | flops | bytes accessed | tf_op | source)
XLA Modules:
  0.0 143.8 jit_solution(2182804619681762066)
XLA Ops:
  3.1 3.3 %all-to-all-start = ((bf16[4,16,640]{2,1,0:T(8,128)(2,1)}), bf16[4,16,640]{2,1,0:T(8,128)(2,1)S(1)}, u32[]{:S(2)}, u32[]{:S(2)}) async-start(bf16[4,16,640]{2,1,0:T(8,128)(2,1)} %pad_maximum_fusion.1), calls=%async_computation | async-start | bytes 163840 | tf_op jit(solution)/shard_map/all_to_all | solution.py:31
  7.1 1.2 fusion.4.own
  8.3 2.4 %collective-permute-start = (bf16[400,768]{1,0:T(8,128)(2,1)S(1)}, bf16[400,768]{1,0:T(8,128)(2,1)S(1)}, u32[]{:S(2)}, u32[]{:S(2)}) collective-permute-start(bf16[400,768]{1,0:T(8,128)(2,1)S(1)} %fusion.4.own), channel_id=1, source_target_pairs={{0,16},{16,0},{1,17},{17,1},{2,18},{18,2},{3,19},{19,3},{4,20},{20... | collective-permute-start | bytes 1843208 | tf_op jit(solution)/shard_map/ppermute | solution.py:27
  10.7 3.5 %collective-permute-start.1 = (bf16[400,768]{1,0:T(8,128)(2,1)S(1)}, bf16[400,768]{1,0:T(8,128)(2,1)S(1)}, u32[]{:S(2)}, u32[]{:S(2)}) collective-permute-start(bf16[400,768]{1,0:T(8,128)(2,1)S(1)} %fusion.4.own), channel_id=1, source_target_pairs={{0,32},{32,0},{1,33},{33,1},{2,34},{34,2},{3,35},{35,3},{4,36},{36... | collective-permute-start | bytes 1843208 | tf_op jit(solution)/shard_map/ppermute | solution.py:27
  14.3 1.9 %collective-permute-start.2 = (bf16[400,768]{1,0:T(8,128)(2,1)S(1)}, bf16[400,768]{1,0:T(8,128)(2,1)S(1)}, u32[]{:S(2)}, u32[]{:S(2)}) collective-permute-start(bf16[400,768]{1,0:T(8,128)(2,1)S(1)} %fusion.4.own), channel_id=1, source_target_pairs={{0,48},{16,32},{32,16},{48,0},{1,49},{17,33},{33,17},{49,1},{2,50}... | collective-permute-start | bytes 1843208 | tf_op jit(solution)/shard_map/ppermute | solution.py:223
  16.8 40.5 %all_gather.9.weights = bf16[768,640]{1,0:T(8,128)(2,1)} all-gather(bf16[64,640]{1,0:T(8,128)(2,1)S(1)} %bitcast.78), channel_id=1, replica_groups=mesh['zh'=4,'zl'=3,'x'=2,'c'=2,'pipe'=16] {'zh','zl'}, dimensions={0}, use_global_device_ids=true | all-gather | bytes 1064960 | tf_op jit(solution)/shard_map/all_gather | solution.py:214
  59.1 6.6 %shard_map.102 = (f32[4,8,128]{2,1,0:T(8,128)}, f32[512,128]{1,0:T(8,128)}, bf16[512,128]{1,0:T(8,128)(2,1)}, bf16[512,768]{1,0:T(8,128)(2,1)}, bf16[512,512]{1,...) custom-call(s32[2]{0:T(128)} %pad_add_fusion.place, ...), custom_call_target="tpu_custom_call" | custom-call | tf_op jit(solution)/shard_map/pallas_call | solution.py:196
  65.7 6.8 %all-gather = f32[16,8,128]{2,1,0:T(8,128)} all-gather(f32[4,8,128]{2,1,0:T(8,128)} %get-tuple-element.23), channel_id=2, replica_groups=mesh['zh'=4,'zl'=3,'x'=2,'c'=2,'pipe'=16] {'x','c'}, dimensions={0}, use_global_device_ids=true | all-gather | bytes 81920 | tf_op jit(solution)/shard_map/all_gather | solution.py:247
  72.5 5.8 %shard_map.103 = (bf16[4,64,640]{2,1,0:T(8,128)(2,1)}, bf16[4,64,640]{2,1,0:T(8,128)(2,1)}, bf16[4,64,640]{2,1,0:T(8,128)(2,1)}, bf16[512,128]{1,0:T(8,128)(2,1)}, bf16[512,512]{1,0:T(8,128)(2,1)}) custom-call(s32[2]{0:T(128)} %pad_add_fusion.place, f32[4,4,8,128]{3,2,1,0:T(8,128)} %bitcast.79, bf16[400,768]{1,0:T(8,128)(2,1)} %copy-done, ...), custom_call_target="tpu_custom_call" | custom-call | tf_op jit(solution)/shard_map/pallas_call | solution.py:196
  78.4 1.7 %convolution_convert_fusion = bf16[512,768]{1,0:T(8,128)(2,1)S(1)} fusion(bf16[512,512]{1,0:T(8,128)(2,1)} %get-tuple-element.34, bf16[768,640]{1,0:T(8,128)(2,1)S(1)} %copy-done.2), kind=kOutput, calls=%fused_computation.3 | convolution fusion | flops 403046400 | bytes 2097152 | tf_op jit(solution)/shard_map/dot_general | solution.py:53
  80.7 2.4 %collective-permute-start.3 = (bf16[2,2,128,768]{3,2,0,1:T(8,128)(2,1)S(1)}, bf16[2,2,128,768]{3,2,0,1:T(8,128)(2,1)S(1)}, u32[]{:S(2)}, u32[]{:S(2)}) collective-permute-start(bf16[2,2,128,768]{3,2,0,1:T(8,128)(2,1)S(1)} %bitcast.73), channel_id=1, source_target_pairs={{0,16},{16,0},{1,17},{17,1},{2,18},{18,2},{3,19},{19,3},{4,20},{20... | collective-permute-start | bytes 2359304 | tf_op jit(solution)/shard_map/ppermute | solution.py:27
  83.1 1.9 %collective-permute-start.7 = (bf16[4,64,640]{2,1,0:T(8,128)(2,1)S(1)}, bf16[4,64,640]{2,1,0:T(8,128)(2,1)S(1)}, u32[]{:S(2)}, u32[]{:S(2)}) collective-permute-start(bf16[4,64,640]{2,1,0:T(8,128)(2,1)S(1)} %copy-done.12), channel_id=1, source_target_pairs={{0,64},{64,128},{128,192},{192,256},{256,320},{320,384},{384,448},... | collective-permute-start | bytes 983048 | tf_op jit(solution)/shard_map/ppermute | solution.py:27
  85.0 5.1 %collective-permute-start.8 = (bf16[4,64,640]{2,1,0:T(8,128)(2,1)S(1)}, bf16[4,64,640]{2,1,0:T(8,128)(2,1)S(1)}, u32[]{:S(2)}, u32[]{:S(2)}) collective-permute-start(bf16[4,64,640]{2,1,0:T(8,128)(2,1)S(1)} %copy-done.11), channel_id=1, source_target_pairs={{0,704},{64,0},{128,64},{192,128},{256,192},{320,256},{384,320},{4... | collective-permute-start | bytes 983048 | tf_op jit(solution)/shard_map/ppermute | solution.py:27
  90.3 5.7 %collective-permute-done.7 = bf16[4,64,640]{2,1,0:T(8,128)(2,1)S(1)} collective-permute-done((bf16[4,64,640]{2,1,0:T(8,128)(2,1)S(1)}, bf16[4,64,640]{2,1,0:T(8,128)(2,1)S(1)}, u32[]{:S(2)}, u32[]{:S(2)}) %collective-permute-start.7) | collective-permute-done | bytes 327712 | tf_op jit(solution)/shard_map/ppermute | solution.py:27
  96.0 1.2 collective-permute-done.8
  98.0 4.2 %all-to-all-start.1 = ((bf16[4,64,640]{2,1,0:T(8,128)(2,1)}), bf16[4,64,640]{2,1,0:T(8,128)(2,1)S(1)}, u32[]{:S(2)}, u32[]{:S(2)}) async-start(bf16[4,64,640]{2,1,0:T(8,128)(2,1)} %add_convert_fusion), calls=%async_computation.1 | async-start | bytes 655360 | tf_op jit(solution)/shard_map/all_to_all | solution.py:31
  103.2 1.3 convert_add_fusion
  104.5 2.6 %collective-permute-start.4 = (bf16[2,128,768]{2,1,0:T(8,128)(2,1)S(1)}, bf16[2,128,768]{2,1,0:T(8,128)(2,1)S(1)}, u32[]{:S(2)}, u32[]{:S(2)}) collective-permute-start(bf16[2,128,768]{2,1,0:T(8,128)(2,1)S(1)} %fusion.15), channel_id=1, source_target_pairs={{0,32},{32,0},{1,33},{33,1},{2,34},{34,2},{3,35},{35,3},{4,36},{36... | collective-permute-start | bytes 1179656 | tf_op jit(solution)/shard_map/ppermute | solution.py:27
  107.3 13.5 %all-to-all-done.1 = bf16[4,64,640]{2,1,0:T(8,128)(2,1)S(1)} async-done(((bf16[4,64,640]{2,1,0:T(8,128)(2,1)}), bf16[4,64,640]{2,1,0:T(8,128)(2,1)S(1)}, u32[]{:S(2)}, u32[]{:S(2)}) %all-to-all-start.1) | async-done | bytes 327712 | tf_op jit(solution)/shard_map/all_to_all | solution.py:31
  121.6 3.5 %all-to-all-start.2 = ((f32[4,16,640]{2,1,0:T(8,128)}), f32[4,16,640]{2,1,0:T(8,128)S(1)}, u32[]{:S(2)}, u32[]{:S(2)}) async-start(f32[4,16,640]{2,1,0:T(8,128)} %bitcast.23), calls=%async_computation.2 | async-start | bytes 327680 | tf_op jit(solution)/shard_map/all_to_all | solution.py:31
  125.8 4.1 %collective-permute-start.5 = (bf16[128,768]{1,0:T(8,128)(2,1)S(1)}, bf16[128,768]{1,0:T(8,128)(2,1)S(1)}, u32[]{:S(2)}, u32[]{:S(2)}) collective-permute-start(bf16[128,768]{1,0:T(8,128)(2,1)S(1)} %get-tuple-element.41), channel_id=1, source_target_pairs={{0,1},{1,2},{2,3},{3,4},{4,5},{5,6},{6,7},{7,8},{8,9},{9,10},{10,1... | collective-permute-start | bytes 589832 | tf_op jit(solution)/shard_map/ppermute | solution.py:27
  129.9 1.9 %collective-permute-start.6 = (bf16[128,768]{1,0:T(8,128)(2,1)S(1)}, bf16[128,768]{1,0:T(8,128)(2,1)S(1)}, u32[]{:S(2)}, u32[]{:S(2)}) collective-permute-start(bf16[128,768]{1,0:T(8,128)(2,1)S(1)} %get-tuple-element.40), channel_id=1, source_target_pairs={{0,15},{1,0},{2,1},{3,2},{4,3},{5,4},{6,5},{7,6},{8,7},{9,8},{10,9... | collective-permute-start | bytes 589832 | tf_op jit(solution)/shard_map/ppermute | solution.py:27
  133.3 1.6 %collective-permute-done.5 = bf16[128,768]{1,0:T(8,128)(2,1)S(1)} collective-permute-done((bf16[128,768]{1,0:T(8,128)(2,1)S(1)}, bf16[128,768]{1,0:T(8,128)(2,1)S(1)}, u32[]{:S(2)}, u32[]{:S(2)}) %collective-permute-start.5) | collective-permute-done | bytes 196640 | tf_op jit(solution)/shard_map/ppermute | solution.py:27
  134.9 7.5 %collective-permute-done.6 = bf16[128,768]{1,0:T(8,128)(2,1)S(1)} collective-permute-done((bf16[128,768]{1,0:T(8,128)(2,1)S(1)}, bf16[128,768]{1,0:T(8,128)(2,1)S(1)}, u32[]{:S(2)}, u32[]{:S(2)}) %collective-permute-start.6) | collective-permute-done | bytes 196640 | tf_op jit(solution)/shard_map/ppermute | solution.py:27
  (66 shorter events, 12.5 us)
Async XLA Ops:
  3.1 7.6 %all-to-all-start = ((bf16[4,16,640]{2,1,0:T(8,128)(2,1)}), bf16[4,16,640]{2,1,0:T(8,128)(2,1)S(1)}, u32[]{:S(2)}, u32[]{:S(2)}) async-start(bf16[4,16,640]{2,1,0:T(8,128)(2,1)} %pad_maximum_fusion.1), calls=%async_computation | async-start | bytes 163840 | tf_op jit(solution)/shard_map/all_to_all | solution.py:31
  8.3 49.0 %copy-start = (bf16[400,768]{1,0:T(8,128)(2,1)}, bf16[400,768]{1,0:T(8,128)(2,1)S(1)}, u32[]{:S(2)}) copy-start(bf16[400,768]{1,0:T(8,128)(2,1)S(1)} %fusion.4.own) | copy-start | bytes 1843204
  8.3 48.9 %collective-permute-start = (bf16[400,768]{1,0:T(8,128)(2,1)S(1)}, bf16[400,768]{1,0:T(8,128)(2,1)S(1)}, u32[]{:S(2)}, u32[]{:S(2)}) collective-permute-start(bf16[400,768]{1,0:T(8,128)(2,1)S(1)} %fusion.4.own), channel_id=1, source_target_pairs={{0,16},{16,0},{1,17},{17,1},{2,18},{18,2},{3,19},{19,3},{4,20},{20... | collective-permute-start | bytes 1843208 | tf_op jit(solution)/shard_map/ppermute | solution.py:27
  10.7 46.6 %collective-permute-start.1 = (bf16[400,768]{1,0:T(8,128)(2,1)S(1)}, bf16[400,768]{1,0:T(8,128)(2,1)S(1)}, u32[]{:S(2)}, u32[]{:S(2)}) collective-permute-start(bf16[400,768]{1,0:T(8,128)(2,1)S(1)} %fusion.4.own), channel_id=1, source_target_pairs={{0,32},{32,0},{1,33},{33,1},{2,34},{34,2},{3,35},{35,3},{4,36},{36... | collective-permute-start | bytes 1843208 | tf_op jit(solution)/shard_map/ppermute | solution.py:27
  14.3 43.0 %collective-permute-start.2 = (bf16[400,768]{1,0:T(8,128)(2,1)S(1)}, bf16[400,768]{1,0:T(8,128)(2,1)S(1)}, u32[]{:S(2)}, u32[]{:S(2)}) collective-permute-start(bf16[400,768]{1,0:T(8,128)(2,1)S(1)} %fusion.4.own), channel_id=1, source_target_pairs={{0,48},{16,32},{32,16},{48,0},{1,49},{17,33},{33,17},{49,1},{2,50}... | collective-permute-start | bytes 1843208 | tf_op jit(solution)/shard_map/ppermute | solution.py:223
  57.3 1.0 copy-start.4
  58.3 0.8 copy-start.5
  72.5 5.8 %copy-start.2 = (bf16[768,640]{1,0:T(8,128)(2,1)S(1)}, bf16[768,640]{1,0:T(8,128)(2,1)}, u32[]{:S(2)}) copy-start(bf16[768,640]{1,0:T(8,128)(2,1)} %all_gather.9.weights) | copy-start | bytes 2949124
  78.3 1.7 %copy-start.10 = (bf16[512,128]{1,0:T(8,128)(2,1)S(1)}, bf16[512,128]{1,0:T(8,128)(2,1)}, u32[]{:S(2)}) copy-start(bf16[512,128]{1,0:T(8,128)(2,1)} %get-tuple-element.33) | copy-start | bytes 393220
  80.6 2.5 %copy-start.12 = (bf16[4,64,640]{2,1,0:T(8,128)(2,1)S(1)}, bf16[4,64,640]{2,1,0:T(8,128)(2,1)}, u32[]{:S(2)}) copy-start(bf16[4,64,640]{2,1,0:T(8,128)(2,1)} %get-tuple-element.36) | copy-start | bytes 983044
  80.6 4.4 %copy-start.11 = (bf16[4,64,640]{2,1,0:T(8,128)(2,1)S(1)}, bf16[4,64,640]{2,1,0:T(8,128)(2,1)}, u32[]{:S(2)}) copy-start(bf16[4,64,640]{2,1,0:T(8,128)(2,1)} %get-tuple-element.37) | copy-start | bytes 983044
  80.6 9.6 %copy-start.1 = (bf16[1,128,768]{2,1,0:T(8,128)(2,1)S(1)}, bf16[1,128,768]{2,1,0:T(8,128)(2,1)}, u32[]{:S(2)}) copy-start(bf16[1,128,768]{2,1,0:T(8,128)(2,1)} %param.8) | copy-start | bytes 589828
  80.6 16.6 %copy-start.9 = (bf16[4,64,640]{2,1,0:T(8,128)(2,1)S(1)}, bf16[4,64,640]{2,1,0:T(8,128)(2,1)}, u32[]{:S(2)}) copy-start(bf16[4,64,640]{2,1,0:T(8,128)(2,1)} %get-tuple-element.35) | copy-start | bytes 983044
  80.7 21.6 %collective-permute-start.3 = (bf16[2,2,128,768]{3,2,0,1:T(8,128)(2,1)S(1)}, bf16[2,2,128,768]{3,2,0,1:T(8,128)(2,1)S(1)}, u32[]{:S(2)}, u32[]{:S(2)}) collective-permute-start(bf16[2,2,128,768]{3,2,0,1:T(8,128)(2,1)S(1)} %bitcast.73), channel_id=1, source_target_pairs={{0,16},{16,0},{1,17},{17,1},{2,18},{18,2},{3,19},{19,3},{4,20},{20... | collective-permute-start | bytes 2359304 | tf_op jit(solution)/shard_map/ppermute | solution.py:27
  83.1 12.9 %collective-permute-start.7 = (bf16[4,64,640]{2,1,0:T(8,128)(2,1)S(1)}, bf16[4,64,640]{2,1,0:T(8,128)(2,1)S(1)}, u32[]{:S(2)}, u32[]{:S(2)}) collective-permute-start(bf16[4,64,640]{2,1,0:T(8,128)(2,1)S(1)} %copy-done.12), channel_id=1, source_target_pairs={{0,64},{64,128},{128,192},{192,256},{256,320},{320,384},{384,448},... | collective-permute-start | bytes 983048 | tf_op jit(solution)/shard_map/ppermute | solution.py:27
  85.0 12.2 %collective-permute-start.8 = (bf16[4,64,640]{2,1,0:T(8,128)(2,1)S(1)}, bf16[4,64,640]{2,1,0:T(8,128)(2,1)S(1)}, u32[]{:S(2)}, u32[]{:S(2)}) collective-permute-start(bf16[4,64,640]{2,1,0:T(8,128)(2,1)S(1)} %copy-done.11), channel_id=1, source_target_pairs={{0,704},{64,0},{128,64},{192,128},{256,192},{320,256},{384,320},{4... | collective-permute-start | bytes 983048 | tf_op jit(solution)/shard_map/ppermute | solution.py:27
  98.0 22.9 %all-to-all-start.1 = ((bf16[4,64,640]{2,1,0:T(8,128)(2,1)}), bf16[4,64,640]{2,1,0:T(8,128)(2,1)S(1)}, u32[]{:S(2)}, u32[]{:S(2)}) async-start(bf16[4,64,640]{2,1,0:T(8,128)(2,1)} %add_convert_fusion), calls=%async_computation.1 | async-start | bytes 655360 | tf_op jit(solution)/shard_map/all_to_all | solution.py:31
  102.3 0.9 copy-start.6
  104.5 20.6 %collective-permute-start.4 = (bf16[2,128,768]{2,1,0:T(8,128)(2,1)S(1)}, bf16[2,128,768]{2,1,0:T(8,128)(2,1)S(1)}, u32[]{:S(2)}, u32[]{:S(2)}) collective-permute-start(bf16[2,128,768]{2,1,0:T(8,128)(2,1)S(1)} %fusion.15), channel_id=1, source_target_pairs={{0,32},{32,0},{1,33},{33,1},{2,34},{34,2},{3,35},{35,3},{4,36},{36... | collective-permute-start | bytes 1179656 | tf_op jit(solution)/shard_map/ppermute | solution.py:27
  121.6 3.9 %copy-start.7 = (bf16[1,128,768]{2,1,0:T(8,128)(2,1)S(1)}, bf16[1,128,768]{2,1,0:T(8,128)(2,1)}, u32[]{:S(2)}) copy-start(bf16[1,128,768]{2,1,0:T(8,128)(2,1)} %param.9) | copy-start | bytes 589828
  121.6 3.9 %copy-start.8 = (bf16[1,128,768]{2,1,0:T(8,128)(2,1)S(1)}, bf16[1,128,768]{2,1,0:T(8,128)(2,1)}, u32[]{:S(2)}) copy-start(bf16[1,128,768]{2,1,0:T(8,128)(2,1)} %param.7) | copy-start | bytes 589828
  121.6 10.3 %all-to-all-start.2 = ((f32[4,16,640]{2,1,0:T(8,128)}), f32[4,16,640]{2,1,0:T(8,128)S(1)}, u32[]{:S(2)}, u32[]{:S(2)}) async-start(f32[4,16,640]{2,1,0:T(8,128)} %bitcast.23), calls=%async_computation.2 | async-start | bytes 327680 | tf_op jit(solution)/shard_map/all_to_all | solution.py:31
  125.8 9.2 %collective-permute-start.5 = (bf16[128,768]{1,0:T(8,128)(2,1)S(1)}, bf16[128,768]{1,0:T(8,128)(2,1)S(1)}, u32[]{:S(2)}, u32[]{:S(2)}) collective-permute-start(bf16[128,768]{1,0:T(8,128)(2,1)S(1)} %get-tuple-element.41), channel_id=1, source_target_pairs={{0,1},{1,2},{2,3},{3,4},{4,5},{5,6},{6,7},{7,8},{8,9},{9,10},{10,1... | collective-permute-start | bytes 589832 | tf_op jit(solution)/shard_map/ppermute | solution.py:27
  129.9 12.5 %collective-permute-start.6 = (bf16[128,768]{1,0:T(8,128)(2,1)S(1)}, bf16[128,768]{1,0:T(8,128)(2,1)S(1)}, u32[]{:S(2)}, u32[]{:S(2)}) collective-permute-start(bf16[128,768]{1,0:T(8,128)(2,1)S(1)} %get-tuple-element.40), channel_id=1, source_target_pairs={{0,15},{1,0},{2,1},{3,2},{4,3},{5,4},{6,5},{7,6},{8,7},{9,8},{10,9... | collective-permute-start | bytes 589832 | tf_op jit(solution)/shard_map/ppermute | solution.py:27
  (1 other events, 0.8 us)

commit v3 on v2

--- a/solution.py
+++ b/solution.py
@@ -77,6 +77,14 @@
     for k, column in enumerate(columns):
         whole = jnp.where(lane == k, column, whole)
     return whole.T[:8]
+
+
+def weights_kernel(proj, out, mine):
+    for h in range(HEADS):
+        for k in range(4):
+            first = k * HID + h * HEAD_DIM
+            mine[h, :, k * HEAD_DIM : (k + 1) * HEAD_DIM] = proj[:, first : first + HEAD_DIM].astype(BF)
+        mine[h, :, 512:] = out[:, h * HEAD_DIM : (h + 1) * HEAD_DIM].astype(BF)
 
 
 def first_kernel(
@@ -199,17 +207,14 @@
         in_specs=[scalar] + [whole] * len(operands),
         out_specs=[whole] * len(shapes),
         scratch_shapes=[pltpu.VMEM(*shape) for shape in scratch],
+        compiler_params=pltpu.CompilerParams(vmem_limit_bytes=24 << 20),
     )(place, *operands)
 
 
 def per_device(acts_fwd, acts_bwd, cotangent, lens_fwd, lens_bwd, w_proj, w_out):
-    mine = jnp.concatenate(
-        [
-            w_proj[0].reshape(16, 4, HEADS, HEAD_DIM).transpose(2, 0, 1, 3).reshape(HEADS, 16, 512),
-            w_out[0].T.reshape(16, HEADS, HEAD_DIM).transpose(1, 0, 2),
-        ],
-        axis=-1,
-    ).astype(BF)
+    mine = pl.pallas_call(
+        weights_kernel, out_shape=jax.ShapeDtypeStruct((HEADS, 16, 640), BF)
+    )(w_proj[0], w_out[0].T)
     group = exchanged(mine).reshape(64, 640)
     weights = lax.all_gather(group, ALONG_Z, axis=0, tiled=True)
 

time: 145 us -> 131 us (0.903)
  Pallas kernels: 12.4 us -> 8.21 us
  blocking collectives: 47.3 us -> 44.1 us
  other arithmetic: 8.67 us -> 5.85 us
  local copies, waits for them, and re-layouts: 5.87 us -> 3.9 us
    pallas_call x2, Pallas kernels: 12.4 us -> 6.65 us  [called(): pl.pallas_call(kernel, out_shape=[jax.ShapeDtypeStruct(*shape) for shape...]
    unnamed x29 -> x11, local copies, waits for them, and re-layouts: 4.18 us -> 2.3 us
    all_gather x1, blocking collectives: 6.8 us -> 5.23 us  [per_device(): every = lax.all_gather(stats, QUAD, axis=0, tiled=False)]
    all_gather x1, blocking collectives: 40.5 us -> 38.9 us  [per_device(): weights = lax.all_gather(group, ALONG_Z, axis=0, tiled=True)]
    pallas_call x0 -> x1, Pallas kernels: none -> 1.55 us  [per_device(): pl.pallas_call(weights_kernel, out_shape=jax.ShapeDtypeStruct((HEADS, 16,...]
  transfers between devices with their start and end apart: 12 -> 12, of which waited for: 5 -> 5; matrix products, arithmetic and copies ran while one was open for 5% -> 6% of each run, Pallas kernels for 0% -> 0%
where the time goes in v3:
time: 131 us; the launch traced here: 130 us
  blocking collectives  44.1 us (34%)
  starting transfers between devices  38 us (29%)
  waiting for transfers between devices  28.5 us (22%)
  Pallas kernels  8.21 us (6%)
  other arithmetic  5.85 us (4%)
  local copies, waits for them, and re-layouts  3.9 us (3%)
    all_gather x1, blocking collectives, per_device(): weights = lax.all_gather(group, ALONG_Z, axis=0, tiled=True)  38.9 us
    ppermute x8, starting transfers between devices, shifted(): lax.ppermute(array, axis, [(i, (i + by) % count) for i in range(count)])  25 us
    ppermute x8, waiting for transfers between devices, shifted(): lax.ppermute(array, axis, [(i, (i + by) % count) for i in range(count)])  15.9 us
    all_to_all x3, waiting for transfers between devices, exchanged(): return lax.all_to_all(array, axis, split_axis=0, concat_axis=0, tiled=True)  12.5 us
    all_to_all x3, starting transfers between devices, exchanged(): return lax.all_to_all(array, axis, split_axis=0, concat_axis=0, tiled=True)  11.1 us
    pallas_call x2, Pallas kernels, called(): pl.pallas_call(kernel, out_shape=[jax.ShapeDtypeStruct(*shape) for shape...  6.65 us
    all_gather x1, blocking collectives, per_device(): every = lax.all_gather(stats, QUAD, axis=0, tiled=False)  5.23 us
  transfers between devices with their start and end apart: 12, of which 5 were waited for; matrix products, arithmetic and copies ran while one was open for 6% of the time, Pallas kernels for 0%

profile of v3, /device:TPU:56, one launch (start us, length us, event | category | flops | bytes accessed | tf_op | source)
XLA Modules:
  0.0 130.5 jit_solution(4184163411383180346)
XLA Ops:
  0.6 1.6 %shard_map.102 = bf16[4,16,640]{2,1,0:T(8,128)(2,1)} custom-call(f32[16,2048]{1,0:T(8,128)} %bitcast.75, f32[16,512]{1,0:T(8,128)} %bitcast.76), custom_call_target="tpu_custom_call" | custom-call | tf_op jit(solution)/shard_map/pallas_call | solution.py:215
  2.2 3.3 %all-to-all-start = ((bf16[4,16,640]{2,1,0:T(8,128)(2,1)}), bf16[4,16,640]{2,1,0:T(8,128)(2,1)S(1)}, u32[]{:S(2)}, u32[]{:S(2)}) async-start(bf16[4,16,640]{2,1,0:T(8,128)(2,1)} %shard_map.102), calls=%async_computation | async-start | bytes 163840 | tf_op jit(solution)/shard_map/all_to_all | solution.py:31
  6.3 1.2 fusion.4.own
  7.4 2.4 %collective-permute-start = (bf16[400,768]{1,0:T(8,128)(2,1)S(1)}, bf16[400,768]{1,0:T(8,128)(2,1)S(1)}, u32[]{:S(2)}, u32[]{:S(2)}) collective-permute-start(bf16[400,768]{1,0:T(8,128)(2,1)S(1)} %fusion.4.own), channel_id=1, source_target_pairs={{0,16},{16,0},{1,17},{17,1},{2,18},{18,2},{3,19},{19,3},{4,20},{20... | collective-permute-start | bytes 1843208 | tf_op jit(solution)/shard_map/ppermute | solution.py:27
  9.8 3.5 %collective-permute-start.1 = (bf16[400,768]{1,0:T(8,128)(2,1)S(1)}, bf16[400,768]{1,0:T(8,128)(2,1)S(1)}, u32[]{:S(2)}, u32[]{:S(2)}) collective-permute-start(bf16[400,768]{1,0:T(8,128)(2,1)S(1)} %fusion.4.own), channel_id=1, source_target_pairs={{0,32},{32,0},{1,33},{33,1},{2,34},{34,2},{3,35},{35,3},{4,36},{36... | collective-permute-start | bytes 1843208 | tf_op jit(solution)/shard_map/ppermute | solution.py:27
  13.4 1.9 %collective-permute-start.2 = (bf16[400,768]{1,0:T(8,128)(2,1)S(1)}, bf16[400,768]{1,0:T(8,128)(2,1)S(1)}, u32[]{:S(2)}, u32[]{:S(2)}) collective-permute-start(bf16[400,768]{1,0:T(8,128)(2,1)S(1)} %fusion.4.own), channel_id=1, source_target_pairs={{0,48},{16,32},{32,16},{48,0},{1,49},{17,33},{33,17},{49,1},{2,50}... | collective-permute-start | bytes 1843208 | tf_op jit(solution)/shard_map/ppermute | solution.py:228
  15.4 38.9 %all_gather.9.weights = bf16[768,640]{1,0:T(8,128)(2,1)S(1)} all-gather(bf16[64,640]{1,0:T(8,128)(2,1)S(1)} %bitcast.72), channel_id=1, replica_groups=mesh['zh'=4,'zl'=3,'x'=2,'c'=2,'pipe'=16] {'zh','zl'}, dimensions={0}, use_global_device_ids=true | all-gather | bytes 1064960 | tf_op jit(solution)/shard_map/all_gather | solution.py:219
  54.3 4.0 %shard_map.103 = (f32[4,8,128]{2,1,0:T(8,128)S(1)}, f32[512,128]{1,0:T(8,128)S(1)}, bf16[512,128]{1,0:T(8,128)(2,1)S(1)}, bf16[512,768]{1,0:T(8,128)(2,1)S(1)}, ...) custom-call(s32[2]{0:T(128)S(1)} %pad_add_fusion.place, ...), custom_call_target="tpu_custom_call" | custom-call | tf_op jit(solution)/shard_map/pallas_call | solution.py:204
  58.3 5.2 %all-gather = f32[16,8,128]{2,1,0:T(8,128)S(1)} all-gather(f32[4,8,128]{2,1,0:T(8,128)S(1)} %get-tuple-element.23), channel_id=2, replica_groups=mesh['zh'=4,'zl'=3,'x'=2,'c'=2,'pipe'=16] {'x','c'}, dimensions={0}, use_global_device_ids=true | all-gather | bytes 81920 | tf_op jit(solution)/shard_map/all_gather | solution.py:252
  63.5 2.7 %shard_map.104 = (bf16[4,64,640]{2,1,0:T(8,128)(2,1)S(1)}, bf16[4,64,640]{2,1,0:T(8,128)(2,1)S(1)}, bf16[4,64,640]{2,1,0:T(8,128)(2,1)S(1)}, bf16[512,128]{1,0:T(8,128)(2,1)S(1)}, bf16[512,512]{1,0:T(8,128)(2,1)S(1)}) custom-call(s32[2]{0:T(128)S(1)} %pad_add_fusion.place, f32[4,4,8,128]{3,2,1,0:T(8,128)S(1)} %bitcast.64, bf16[400,768]{1,0:T(8,128)(2,1)S(1)} %fusion.4.own, ...), custom_call_target="tpu_custom_call" | custom-call | tf_op jit(solution)/shard_map/pallas_call | solution.py:204
  67.4 2.4 %collective-permute-start.3 = (bf16[2,2,128,768]{3,2,0,1:T(8,128)(2,1)S(1)}, bf16[2,2,128,768]{3,2,0,1:T(8,128)(2,1)S(1)}, u32[]{:S(2)}, u32[]{:S(2)}) collective-permute-start(bf16[2,2,128,768]{3,2,0,1:T(8,128)(2,1)S(1)} %bitcast.67), channel_id=1, source_target_pairs={{0,16},{16,0},{1,17},{17,1},{2,18},{18,2},{3,19},{19,3},{4,20},{20... | collective-permute-start | bytes 2359304 | tf_op jit(solution)/shard_map/ppermute | solution.py:27
  69.8 1.9 %collective-permute-start.7 = (bf16[4,64,640]{2,1,0:T(8,128)(2,1)S(1)}, bf16[4,64,640]{2,1,0:T(8,128)(2,1)S(1)}, u32[]{:S(2)}, u32[]{:S(2)}) collective-permute-start(bf16[4,64,640]{2,1,0:T(8,128)(2,1)S(1)} %get-tuple-element.36), channel_id=1, source_target_pairs={{0,64},{64,128},{128,192},{192,256},{256,320},{320,384},{384,448},... | collective-permute-start | bytes 983048 | tf_op jit(solution)/shard_map/ppermute | solution.py:27
  71.7 5.1 %collective-permute-start.8 = (bf16[4,64,640]{2,1,0:T(8,128)(2,1)S(1)}, bf16[4,64,640]{2,1,0:T(8,128)(2,1)S(1)}, u32[]{:S(2)}, u32[]{:S(2)}) collective-permute-start(bf16[4,64,640]{2,1,0:T(8,128)(2,1)S(1)} %get-tuple-element.37), channel_id=1, source_target_pairs={{0,704},{64,0},{128,64},{192,128},{256,192},{320,256},{384,320},{4... | collective-permute-start | bytes 983048 | tf_op jit(solution)/shard_map/ppermute | solution.py:27
  77.0 5.7 %collective-permute-done.7 = bf16[4,64,640]{2,1,0:T(8,128)(2,1)S(1)} collective-permute-done((bf16[4,64,640]{2,1,0:T(8,128)(2,1)S(1)}, bf16[4,64,640]{2,1,0:T(8,128)(2,1)S(1)}, u32[]{:S(2)}, u32[]{:S(2)}) %collective-permute-start.7) | collective-permute-done | bytes 327712 | tf_op jit(solution)/shard_map/ppermute | solution.py:27
  82.7 1.2 collective-permute-done.8
  84.7 4.3 %all-to-all-start.1 = ((bf16[4,64,640]{2,1,0:T(8,128)(2,1)}), bf16[4,64,640]{2,1,0:T(8,128)(2,1)S(1)}, u32[]{:S(2)}, u32[]{:S(2)}) async-start(bf16[4,64,640]{2,1,0:T(8,128)(2,1)} %add_convert_fusion), calls=%async_computation.1 | async-start | bytes 655360 | tf_op jit(solution)/shard_map/all_to_all | solution.py:31
  89.9 1.3 convert_add_fusion
  91.2 3.6 %collective-permute-start.4 = (bf16[2,128,768]{2,1,0:T(8,128)(2,1)S(1)}, bf16[2,128,768]{2,1,0:T(8,128)(2,1)S(1)}, u32[]{:S(2)}, u32[]{:S(2)}) collective-permute-start(bf16[2,128,768]{2,1,0:T(8,128)(2,1)S(1)} %fusion.15), channel_id=1, source_target_pairs={{0,32},{32,0},{1,33},{33,1},{2,34},{34,2},{3,35},{35,3},{4,36},{36... | collective-permute-start | bytes 1179656 | tf_op jit(solution)/shard_map/ppermute | solution.py:27
  95.1 12.5 %all-to-all-done.1 = bf16[4,64,640]{2,1,0:T(8,128)(2,1)S(1)} async-done(((bf16[4,64,640]{2,1,0:T(8,128)(2,1)}), bf16[4,64,640]{2,1,0:T(8,128)(2,1)S(1)}, u32[]{:S(2)}, u32[]{:S(2)}) %all-to-all-start.1) | async-done | bytes 327712 | tf_op jit(solution)/shard_map/all_to_all | solution.py:31
  108.3 3.5 %all-to-all-start.2 = ((f32[4,16,640]{2,1,0:T(8,128)}), f32[4,16,640]{2,1,0:T(8,128)S(1)}, u32[]{:S(2)}, u32[]{:S(2)}) async-start(f32[4,16,640]{2,1,0:T(8,128)} %bitcast.22), calls=%async_computation.2 | async-start | bytes 327680 | tf_op jit(solution)/shard_map/all_to_all | solution.py:31
  112.5 4.1 %collective-permute-start.5 = (bf16[128,768]{1,0:T(8,128)(2,1)S(1)}, bf16[128,768]{1,0:T(8,128)(2,1)S(1)}, u32[]{:S(2)}, u32[]{:S(2)}) collective-permute-start(bf16[128,768]{1,0:T(8,128)(2,1)S(1)} %get-tuple-element.41), channel_id=1, source_target_pairs={{0,1},{1,2},{2,3},{3,4},{4,5},{5,6},{6,7},{7,8},{8,9},{9,10},{10,1... | collective-permute-start | bytes 589832 | tf_op jit(solution)/shard_map/ppermute | solution.py:27
  116.7 1.9 %collective-permute-start.6 = (bf16[128,768]{1,0:T(8,128)(2,1)S(1)}, bf16[128,768]{1,0:T(8,128)(2,1)S(1)}, u32[]{:S(2)}, u32[]{:S(2)}) collective-permute-start(bf16[128,768]{1,0:T(8,128)(2,1)S(1)} %get-tuple-element.40), channel_id=1, source_target_pairs={{0,15},{1,0},{2,1},{3,2},{4,3},{5,4},{6,5},{7,6},{8,7},{9,8},{10,9... | collective-permute-start | bytes 589832 | tf_op jit(solution)/shard_map/ppermute | solution.py:27
  120.1 1.6 %collective-permute-done.5 = bf16[128,768]{1,0:T(8,128)(2,1)S(1)} collective-permute-done((bf16[128,768]{1,0:T(8,128)(2,1)S(1)}, bf16[128,768]{1,0:T(8,128)(2,1)S(1)}, u32[]{:S(2)}, u32[]{:S(2)}) %collective-permute-start.5) | collective-permute-done | bytes 196640 | tf_op jit(solution)/shard_map/ppermute | solution.py:27
  121.7 7.5 %collective-permute-done.6 = bf16[128,768]{1,0:T(8,128)(2,1)S(1)} collective-permute-done((bf16[128,768]{1,0:T(8,128)(2,1)S(1)}, bf16[128,768]{1,0:T(8,128)(2,1)S(1)}, u32[]{:S(2)}, u32[]{:S(2)}) %collective-permute-start.6) | collective-permute-done | bytes 196640 | tf_op jit(solution)/shard_map/ppermute | solution.py:27
  (43 shorter events, 8.3 us)
Async XLA Ops:
  2.2 7.6 %all-to-all-start = ((bf16[4,16,640]{2,1,0:T(8,128)(2,1)}), bf16[4,16,640]{2,1,0:T(8,128)(2,1)S(1)}, u32[]{:S(2)}, u32[]{:S(2)}) async-start(bf16[4,16,640]{2,1,0:T(8,128)(2,1)} %shard_map.102), calls=%async_computation | async-start | bytes 163840 | tf_op jit(solution)/shard_map/all_to_all | solution.py:31
  7.4 46.9 %collective-permute-start = (bf16[400,768]{1,0:T(8,128)(2,1)S(1)}, bf16[400,768]{1,0:T(8,128)(2,1)S(1)}, u32[]{:S(2)}, u32[]{:S(2)}) collective-permute-start(bf16[400,768]{1,0:T(8,128)(2,1)S(1)} %fusion.4.own), channel_id=1, source_target_pairs={{0,16},{16,0},{1,17},{17,1},{2,18},{18,2},{3,19},{19,3},{4,20},{20... | collective-permute-start | bytes 1843208 | tf_op jit(solution)/shard_map/ppermute | solution.py:27
  9.8 44.5 %collective-permute-start.1 = (bf16[400,768]{1,0:T(8,128)(2,1)S(1)}, bf16[400,768]{1,0:T(8,128)(2,1)S(1)}, u32[]{:S(2)}, u32[]{:S(2)}) collective-permute-start(bf16[400,768]{1,0:T(8,128)(2,1)S(1)} %fusion.4.own), channel_id=1, source_target_pairs={{0,32},{32,0},{1,33},{33,1},{2,34},{34,2},{3,35},{35,3},{4,36},{36... | collective-permute-start | bytes 1843208 | tf_op jit(solution)/shard_map/ppermute | solution.py:27
  13.4 40.9 %collective-permute-start.2 = (bf16[400,768]{1,0:T(8,128)(2,1)S(1)}, bf16[400,768]{1,0:T(8,128)(2,1)S(1)}, u32[]{:S(2)}, u32[]{:S(2)}) collective-permute-start(bf16[400,768]{1,0:T(8,128)(2,1)S(1)} %fusion.4.own), channel_id=1, source_target_pairs={{0,48},{16,32},{32,16},{48,0},{1,49},{17,33},{33,17},{49,1},{2,50}... | collective-permute-start | bytes 1843208 | tf_op jit(solution)/shard_map/ppermute | solution.py:228
  67.3 9.5 %copy-start = (bf16[1,128,768]{2,1,0:T(8,128)(2,1)S(1)}, bf16[1,128,768]{2,1,0:T(8,128)(2,1)}, u32[]{:S(2)}) copy-start(bf16[1,128,768]{2,1,0:T(8,128)(2,1)} %param.8) | copy-start | bytes 589828
  67.4 21.6 %collective-permute-start.3 = (bf16[2,2,128,768]{3,2,0,1:T(8,128)(2,1)S(1)}, bf16[2,2,128,768]{3,2,0,1:T(8,128)(2,1)S(1)}, u32[]{:S(2)}, u32[]{:S(2)}) collective-permute-start(bf16[2,2,128,768]{3,2,0,1:T(8,128)(2,1)S(1)} %bitcast.67), channel_id=1, source_target_pairs={{0,16},{16,0},{1,17},{17,1},{2,18},{18,2},{3,19},{19,3},{4,20},{20... | collective-permute-start | bytes 2359304 | tf_op jit(solution)/shard_map/ppermute | solution.py:27
  69.8 12.9 %collective-permute-start.7 = (bf16[4,64,640]{2,1,0:T(8,128)(2,1)S(1)}, bf16[4,64,640]{2,1,0:T(8,128)(2,1)S(1)}, u32[]{:S(2)}, u32[]{:S(2)}) collective-permute-start(bf16[4,64,640]{2,1,0:T(8,128)(2,1)S(1)} %get-tuple-element.36), channel_id=1, source_target_pairs={{0,64},{64,128},{128,192},{192,256},{256,320},{320,384},{384,448},... | collective-permute-start | bytes 983048 | tf_op jit(solution)/shard_map/ppermute | solution.py:27
  71.7 12.1 %collective-permute-start.8 = (bf16[4,64,640]{2,1,0:T(8,128)(2,1)S(1)}, bf16[4,64,640]{2,1,0:T(8,128)(2,1)S(1)}, u32[]{:S(2)}, u32[]{:S(2)}) collective-permute-start(bf16[4,64,640]{2,1,0:T(8,128)(2,1)S(1)} %get-tuple-element.37), channel_id=1, source_target_pairs={{0,704},{64,0},{128,64},{192,128},{256,192},{320,256},{384,320},{4... | collective-permute-start | bytes 983048 | tf_op jit(solution)/shard_map/ppermute | solution.py:27
  84.7 22.9 %all-to-all-start.1 = ((bf16[4,64,640]{2,1,0:T(8,128)(2,1)}), bf16[4,64,640]{2,1,0:T(8,128)(2,1)S(1)}, u32[]{:S(2)}, u32[]{:S(2)}) async-start(bf16[4,64,640]{2,1,0:T(8,128)(2,1)} %add_convert_fusion), calls=%async_computation.1 | async-start | bytes 655360 | tf_op jit(solution)/shard_map/all_to_all | solution.py:31
  89.0 0.9 copy-start.1
  91.2 20.6 %collective-permute-start.4 = (bf16[2,128,768]{2,1,0:T(8,128)(2,1)S(1)}, bf16[2,128,768]{2,1,0:T(8,128)(2,1)S(1)}, u32[]{:S(2)}, u32[]{:S(2)}) collective-permute-start(bf16[2,128,768]{2,1,0:T(8,128)(2,1)S(1)} %fusion.15), channel_id=1, source_target_pairs={{0,32},{32,0},{1,33},{33,1},{2,34},{34,2},{3,35},{35,3},{4,36},{36... | collective-permute-start | bytes 1179656 | tf_op jit(solution)/shard_map/ppermute | solution.py:27
  108.3 3.9 %copy-start.2 = (bf16[1,128,768]{2,1,0:T(8,128)(2,1)S(1)}, bf16[1,128,768]{2,1,0:T(8,128)(2,1)}, u32[]{:S(2)}) copy-start(bf16[1,128,768]{2,1,0:T(8,128)(2,1)} %param.9) | copy-start | bytes 589828
  108.3 3.9 %copy-start.3 = (bf16[1,128,768]{2,1,0:T(8,128)(2,1)S(1)}, bf16[1,128,768]{2,1,0:T(8,128)(2,1)}, u32[]{:S(2)}) copy-start(bf16[1,128,768]{2,1,0:T(8,128)(2,1)} %param.7) | copy-start | bytes 589828
  108.3 10.2 %all-to-all-start.2 = ((f32[4,16,640]{2,1,0:T(8,128)}), f32[4,16,640]{2,1,0:T(8,128)S(1)}, u32[]{:S(2)}, u32[]{:S(2)}) async-start(f32[4,16,640]{2,1,0:T(8,128)} %bitcast.22), calls=%async_computation.2 | async-start | bytes 327680 | tf_op jit(solution)/shard_map/all_to_all | solution.py:31
  112.5 9.2 %collective-permute-start.5 = (bf16[128,768]{1,0:T(8,128)(2,1)S(1)}, bf16[128,768]{1,0:T(8,128)(2,1)S(1)}, u32[]{:S(2)}, u32[]{:S(2)}) collective-permute-start(bf16[128,768]{1,0:T(8,128)(2,1)S(1)} %get-tuple-element.41), channel_id=1, source_target_pairs={{0,1},{1,2},{2,3},{3,4},{4,5},{5,6},{6,7},{7,8},{8,9},{9,10},{10,1... | collective-permute-start | bytes 589832 | tf_op jit(solution)/shard_map/ppermute | solution.py:27
  116.7 12.5 %collective-permute-start.6 = (bf16[128,768]{1,0:T(8,128)(2,1)S(1)}, bf16[128,768]{1,0:T(8,128)(2,1)S(1)}, u32[]{:S(2)}, u32[]{:S(2)}) collective-permute-start(bf16[128,768]{1,0:T(8,128)(2,1)S(1)} %get-tuple-element.40), channel_id=1, source_target_pairs={{0,15},{1,0},{2,1},{3,2},{4,3},{5,4},{6,5},{7,6},{8,7},{9,8},{10,9... | collective-permute-start | bytes 589832 | tf_op jit(solution)/shard_map/ppermute | solution.py:27
